TPU v7x, 256 devices: a whole 4x4x8 slice. The times are simulated.
256 devices in a mesh: gz: 64 (over x, z, core), gx: 4 (over y).
Axes of the slice: x: 4, y: 4, z: 8, core: 2. Of those that a mesh axis runs over, the one named last changes fastest.
Arguments:
- strength: float32 [3, 131072], P(None, ('gz', 'gx')), may hold values from -6 to 6
- offsets: float32 [3, 131072], P(None, ('gz', 'gx')), may hold values from -0.5 to 0.5
- cell_index: int32 [131072], P(('gz', 'gx')), may hold values from 0 to 131071
- migrate_count: int32 [64, 4, 2], P('gz', 'gx'), may hold values from 32 to 64, as said below
- ambient: float32 [3, 512, 256, 256], P(None, 'gz', 'gx'), may hold values from -2.5 to 2.5
Outputs:
- velocity: float32 [3, 512, 256, 256], P(None, 'gz', 'gx')
- vorticity: float32 [3, 512, 256, 256], P(None, 'gz', 'gx')
Inputs may be any that keep to these rules, and one draw needn't show every extreme that they name: `migrate_count`: some device has 64 in the first entry and some device has 64 in the second.
All inputs are finite; a program needn't handle non-finite values.
Results may differ from a plain program's by a relative error of at most 0.0003.
Values sent between devices are 32-bit elements; how exact they have to be, the bound alone decides.
A program may use at most 128 MiB of HBM per device.

v0:
```python
import math

import jax
import jax.numpy as jnp
from jax import lax
from jax.sharding import PartitionSpec as P

NX = 256
NY = 256
PART = 512
MIG = 64


time_step = 0.25
highest = lax.Precision.HIGHEST


def padded_2(cells, sides, width):
    for axis, dim in sides:
        count = lax.axis_size(axis)
        head = lax.slice_in_dim(cells, 0, width, axis=dim)
        tail = lax.slice_in_dim(cells, cells.shape[dim] - width, cells.shape[dim], axis=dim)
        cells = jnp.concatenate(
            [
                lax.ppermute(tail, axis, [(i, (i + 1) % count) for i in range(count)]),
                cells,
                lax.ppermute(head, axis, [((i + 1) % count, i) for i in range(count)]),
            ],
            axis=dim,
        )
    return cells


def kernel_weight(distance):
    radius = jnp.abs(distance)
    near_part = 1.0 - 2.5 * radius * radius + 1.5 * radius * radius * radius
    far_part = 0.5 * (2.0 - radius) * (2.0 - radius) * (1.0 - radius)
    return jnp.where(radius < 1.0, near_part, jnp.where(radius < 2.0, far_part, 0.0))


def wave_of(position, extent):
    signed = jnp.where(position < extent // 2, position, position - extent)
    return 2.0 * jnp.pi * signed.astype(jnp.float32) / extent


def fourier_tables(extent):
    position = jnp.arange(extent, dtype=jnp.int32)
    phase = position[:, None] * position[None, :] % extent
    angle = 2.0 * jnp.pi * phase.astype(jnp.float32) / extent
    return (jnp.cos(angle), jnp.sin(angle))


def complex_table(extent, direction):
    cosine, sine = fourier_tables(extent)
    real_rows = jnp.stack([cosine, -direction * sine], axis=1)
    imag_rows = jnp.stack([direction * sine, cosine], axis=1)
    return jnp.stack([real_rows, imag_rows], axis=0)


def split_pairs(values):
    return values.reshape(values.shape[:-1] + (2, values.shape[-1] // 2))


def join_pairs(values):
    return values.reshape(values.shape[:-2] + (values.shape[-2] * values.shape[-1],))


def lateral_table(extent, pencil_count, mode_count):
    column = jnp.arange(2 * mode_count * pencil_count, dtype=jnp.int32)
    wave_number = column // (2 * mode_count) * mode_count + column % mode_count
    half_flag = column // mode_count % 2
    position = jnp.arange(extent, dtype=jnp.int32)
    phase = position[:, None] * wave_number[None, :] % extent
    angle = 2.0 * jnp.pi * phase.astype(jnp.float32) / extent
    return (jnp.where(half_flag[None, :] == 0, jnp.cos(angle), -jnp.sin(angle)), wave_number)


def halved_tables(extent, pencil_count):
    mode_count = extent // (2 * pencil_count)
    table, wave_number = lateral_table(extent, pencil_count, mode_count)
    column = jnp.arange(table.shape[1], dtype=jnp.int32)
    position = jnp.arange(extent, dtype=jnp.int32)
    alternating = (1 - 2 * (position % 2)).astype(jnp.float32)
    table = jnp.where(column[None, :] == mode_count, alternating[:, None], table)
    weights = jnp.where(wave_number == 0, 1.0, 2.0).astype(jnp.float32)
    return (table, table.T * weights[:, None] * (1.0 / extent))


def times_minus_i(values):
    half_width = values.shape[-1] // 2
    signs = jnp.where(jnp.arange(2 * half_width) < half_width, 1.0, -1.0).astype(jnp.float32)
    return jnp.roll(values, half_width, axis=values.ndim - 1) * signs


def mirrored(values, axis_number):
    return jnp.roll(jnp.flip(values, axis=axis_number), 1, axis=axis_number)


def reslot(values, pencil_index):
    mode_count = values.shape[3] // 2
    middle = values.shape[2] // 2
    real_part = values[..., 0]
    imag_part = values[..., mode_count]
    mirror_real = mirrored(real_part, 2)
    mirror_imag = mirrored(imag_part, 2)
    wave_index = jnp.arange(values.shape[2], dtype=jnp.int32)[None, None, :]
    self_paired = (wave_index == 0) | (wave_index == middle)
    new_real = jnp.where(
        wave_index <= middle, 0.5 * (real_part + mirror_real), 0.5 * (imag_part + mirror_imag)
    )
    new_imag = jnp.where(
        self_paired,
        imag_part,
        jnp.where(
            wave_index < middle, 0.5 * (imag_part - mirror_imag), 0.5 * (real_part - mirror_real)
        ),
    )
    first_pencil = pencil_index == 0
    values = values.at[..., 0].set(jnp.where(first_pencil, new_real, real_part))
    return values.at[..., mode_count].set(jnp.where(first_pencil, new_imag, imag_part))


def unslot(values, pencil_index):
    mode_count = values.shape[3] // 2
    middle = values.shape[2] // 2
    real_part = values[..., 0]
    imag_part = values[..., mode_count]
    mirror_real = mirrored(real_part, 2)
    mirror_imag = mirrored(imag_part, 2)
    wave_index = jnp.arange(values.shape[2], dtype=jnp.int32)[None, None, :]
    self_paired = (wave_index == 0) | (wave_index == middle)
    new_real = jnp.where(
        self_paired,
        real_part,
        jnp.where(wave_index < middle, real_part - mirror_imag, mirror_real + imag_part),
    )
    new_imag = jnp.where(
        self_paired,
        imag_part,
        jnp.where(wave_index < middle, imag_part + mirror_real, real_part - mirror_imag),
    )
    first_pencil = pencil_index == 0
    values = values.at[..., 0].set(jnp.where(first_pencil, new_real, real_part))
    return values.at[..., mode_count].set(jnp.where(first_pencil, new_imag, imag_part))


def curl_modes(spectral, wave_z, wave_x, wave_y, inverse_sq):
    stream = spectral * inverse_sq
    crossed = jnp.stack(
        [
            wave_x * stream[2] - wave_y * stream[1],
            wave_y * stream[0] - wave_z * stream[2],
            wave_z * stream[1] - wave_x * stream[0],
        ]
    )
    return -times_minus_i(crossed)


def packed_velocity(spectral, slab_index, pencil_index, block_width, wake_cells):
    column_pairs = spectral.shape[3]
    mode_count = column_pairs // 2
    z_index = jnp.arange(wake_cells, dtype=jnp.int32)[:, None, None]
    x_global = (slab_index * block_width + jnp.arange(block_width, dtype=jnp.int32))[None, :, None]
    column = jnp.arange(column_pairs, dtype=jnp.int32)[None, None, :]
    y_mode = pencil_index * mode_count + column % mode_count
    packed_column = (pencil_index == 0) & (column % mode_count == 0)
    nyquist = packed_column & (x_global > NX // 2)
    x_mode = jnp.where(nyquist, NX - x_global, x_global)
    wave_z = wave_of(z_index, wake_cells)
    wave_x = wave_of(x_mode, NX)
    wave_y = wave_of(y_mode, NY)
    wave_sq = (
        wave_z * wave_z + wave_x * wave_x + jnp.where(nyquist, jnp.pi * jnp.pi, wave_y * wave_y)
    )
    anchor = (z_index == 0) & (x_mode == 0) & (y_mode == 0) & jnp.logical_not(nyquist)
    inverse_sq = jnp.where(anchor, 0.0, 1.0 / jnp.where(anchor, 1.0, wave_sq))
    trim_z = jnp.where(z_index == wake_cells // 2, 0.0, wave_z)
    trim_x = jnp.where(x_mode == NX // 2, 0.0, wave_x)
    trim_y = jnp.where(nyquist, 0.0, wave_y)
    velocity_hat = curl_modes(spectral, trim_z, trim_x, trim_y, inverse_sq)
    real_part = spectral[..., 0]
    imag_part = spectral[..., mode_count]
    mirror_real = mirrored(real_part, 1)
    mirror_imag = mirrored(imag_part, 1)
    even_pack = jnp.stack(
        [0.5 * (real_part + mirror_real), 0.5 * (imag_part - mirror_imag)], axis=3
    )
    odd_pack = jnp.stack([0.5 * (imag_part + mirror_imag), 0.5 * (mirror_real - real_part)], axis=3)
    plane_z = z_index[:, :, 0]
    x_plane = x_global[:, :, 0]
    pair_wave_z = wave_of(plane_z, wake_cells)
    pair_wave_x = wave_of(x_plane, NX)
    base_sq = pair_wave_z * pair_wave_z + pair_wave_x * pair_wave_x
    pair_anchor = (plane_z == 0) & (x_plane == 0)
    even_inverse = jnp.where(pair_anchor, 0.0, 1.0 / jnp.where(pair_anchor, 1.0, base_sq))[
        ..., None
    ]
    odd_inverse = (1.0 / (base_sq + jnp.pi * jnp.pi))[..., None]
    pair_trim_z = jnp.where(plane_z == wake_cells // 2, 0.0, pair_wave_z)[..., None]
    nothing = jnp.zeros((1, 1, 1), jnp.float32)
    even_hat = curl_modes(even_pack, pair_trim_z, nothing, nothing, even_inverse)
    odd_hat = curl_modes(odd_pack, pair_trim_z, nothing, nothing, odd_inverse)
    joined_real = even_hat[..., 0] - odd_hat[..., 1]
    joined_imag = even_hat[..., 1] + odd_hat[..., 0]
    paired = (pencil_index == 0) & ((x_plane == 0) | (x_plane == NX // 2))
    velocity_hat = velocity_hat.at[..., 0].set(jnp.where(paired, joined_real, velocity_hat[..., 0]))
    return velocity_hat.at[..., mode_count].set(
        jnp.where(paired, joined_imag, velocity_hat[..., mode_count])
    )


def on_device(strength, offsets, cell_index, migrate_count, ambient):
    slab_planes = ambient.shape[1]
    pencil_cols = ambient.shape[2]
    slab_count = lax.axis_size("gz")
    pencil_count = lax.axis_size("gx")
    wake_cells = slab_planes * slab_count
    pencil_index = lax.axis_index("gx")
    up_count = migrate_count[0, 0, 0]
    down_count = migrate_count[0, 0, 1]
    slot_index = jnp.arange(PART, dtype=jnp.int32)
    packet = jnp.concatenate([strength, offsets, cell_index.astype(jnp.float32)[None, :]], axis=0)
    is_strength = (jnp.arange(7) < 3)[:, None]
    head_live = slot_index[:MIG] < up_count
    upward = jnp.where(is_strength & ~head_live[None, :], 0.0, packet[:, :MIG])
    downward = lax.dynamic_slice_in_dim(packet, up_count, MIG, axis=1)
    down_live = jnp.arange(MIG, dtype=jnp.int32) < down_count
    downward = jnp.where(is_strength & ~down_live[None, :], 0.0, downward)
    outgoing = jnp.concatenate([downward, upward], axis=1)
    extended = padded_2(outgoing, (("gz", 1),), MIG)
    arrived = jnp.concatenate([extended[:, :MIG], extended[:, 3 * MIG :]], axis=1)
    staying = slot_index >= up_count + down_count
    retained = jnp.where(is_strength & ~staying[None, :], 0.0, packet)
    particles = jnp.concatenate([retained, arrived], axis=1)
    particle_total = particles.shape[1]
    block_rows = math.gcd(particle_total, 256)
    row_blocks = particles.T.reshape(particle_total // block_rows, block_rows, 7)
    planes = jnp.arange(slab_planes + 4, dtype=jnp.int32) - 2
    columns = jnp.arange(pencil_cols + 4, dtype=jnp.int32) - 2
    lateral = jnp.arange(NY, dtype=jnp.int32)

    def deposit(deposited, row_group):
        cell_ids = row_group[:, 6].astype(jnp.int32)
        z_cell = cell_ids // (pencil_cols * NY)
        x_cell = cell_ids // NY % pencil_cols
        y_cell = cell_ids % NY
        weight_z = kernel_weight(
            (planes[None, :] - z_cell[:, None]).astype(jnp.float32) - row_group[:, 3:4]
        )
        weight_x = kernel_weight(
            (columns[None, :] - x_cell[:, None]).astype(jnp.float32) - row_group[:, 4:5]
        )
        y_offset = (lateral[None, :] - y_cell[:, None] + NY // 2) % NY - NY // 2
        weight_y = kernel_weight(y_offset.astype(jnp.float32) - row_group[:, 5:6])
        spread = (
            row_group[:, 0:3, None, None] * weight_z[:, None, :, None] * weight_x[:, None, None, :]
        )
        spread = spread.reshape(block_rows, -1)
        added = lax.dot_general(
            spread,
            weight_y,
            (((0,), (0,)), ((), ())),
            precision=highest,
            preferred_element_type=jnp.float32,
        )
        return (deposited + added, None)

    start_mesh = jnp.zeros((3 * (slab_planes + 4) * (pencil_cols + 4), NY), jnp.float32)
    deposited, _ = lax.scan(deposit, start_mesh, row_blocks)
    deposited = deposited.reshape(3, slab_planes + 4, pencil_cols + 4, NY)
    plane_rim = jnp.concatenate([deposited[:, :2], deposited[:, slab_planes + 2 :]], axis=1)
    plane_rim = padded_2(plane_rim, (("gz", 1),), 2)
    interior = deposited[:, 2 : slab_planes + 2]
    interior = (
        interior.at[:, :2].add(plane_rim[:, :2]).at[:, slab_planes - 2 :].add(plane_rim[:, 6:])
    )
    column_rim = jnp.concatenate([interior[:, :, :2], interior[:, :, pencil_cols + 2 :]], axis=2)
    column_rim = padded_2(column_rim, (("gx", 2),), 2)
    interior = interior[:, :, 2 : pencil_cols + 2]
    interior = (
        interior.at[:, :, :2]
        .add(column_rim[:, :, :2])
        .at[:, :, pencil_cols - 2 :]
        .add(column_rim[:, :, 6:])
    )
    vorticity_mesh = ambient + interior
    table_y, table_back = halved_tables(NY, pencil_count)
    spectral = jnp.einsum("bzxy,yc->bzxc", vorticity_mesh, table_y, precision=highest)
    ahead_x_table = complex_table(NX, -1.0)
    ahead_z_table = complex_table(wake_cells, -1.0)
    back_x_table = complex_table(NX, 1.0)
    back_z_table = complex_table(wake_cells, 1.0)
    result = join_pairs(
        jnp.einsum(
            "qkrx,bzxrm->bzkqm",
            ahead_x_table,
            split_pairs(lax.all_to_all(spectral, "gx", split_axis=3, concat_axis=2, tiled=True)),
            precision=highest,
        )
    )
    result = reslot(result, pencil_index)
    spectral = result
    block_width = NX // slab_count
    spectral = join_pairs(
        jnp.einsum(
            "qkrz,bzxrm->bkxqm",
            ahead_z_table,
            split_pairs(lax.all_to_all(spectral, "gz", split_axis=2, concat_axis=1, tiled=True)),
            precision=highest,
        )
    )
    velocity_hat = packed_velocity(
        spectral, lax.axis_index("gz"), pencil_index, block_width, wake_cells
    )
    physical = join_pairs(
        jnp.einsum("qkrz,bzxrm->bkxqm", back_z_table, split_pairs(velocity_hat), precision=highest)
    ) * (1.0 / wake_cells)
    pieces = lax.all_to_all(physical, "gz", split_axis=1, concat_axis=2, tiled=True)
    pieces = unslot(pieces, pencil_index)
    physical = join_pairs(
        jnp.einsum("qkrx,bzxrm->bzkqm", back_x_table, split_pairs(pieces), precision=highest)
    ) * (1.0 / NX)
    velocity = jnp.einsum(
        "bzxc,cy->bzxy",
        lax.all_to_all(physical, "gx", split_axis=2, concat_axis=3, tiled=True),
        table_back,
        precision=highest,
    )
    padded = padded_2(velocity, (("gz", 1), ("gx", 2)), 1)
    along_z = (padded[:, 2:, 1:-1] - padded[:, :-2, 1:-1]) * 0.5
    along_x = (padded[:, 1:-1, 2:] - padded[:, 1:-1, :-2]) * 0.5
    along_y = (jnp.roll(velocity, -1, axis=3) - jnp.roll(velocity, 1, axis=3)) * 0.5
    stretch = (
        vorticity_mesh[0] * along_z + vorticity_mesh[1] * along_x + vorticity_mesh[2] * along_y
    )
    return (velocity, vorticity_mesh + time_step * stretch)


def solution(mesh):
    placed = (
        P(None, ("gz", "gx")),
        P(None, ("gz", "gx")),
        P(("gz", "gx")),
        P("gz", "gx", None),
        P(None, "gz", "gx", None),
    )
    return jax.shard_map(
        on_device,
        mesh=mesh,
        in_specs=placed,
        out_specs=(P(None, "gz", "gx", None), P(None, "gz", "gx", None)),
        check_vma=False,
    )
```

profile of v0, /device:TPU:8, one launch (start us, length us, event | category | flops | bytes accessed | tf_op | source)
XLA Modules:
  0.0 575.8 jit_solution(1345845632013300558)
XLA Ops:
  8.1 7.6 %collective-permute-start.1 = (f32[7,64]{1,0:T(8,128)S(1)}, f32[7,64]{1,0:T(8,128)S(1)}, u32[]{:S(2)}, u32[]{:S(2)}) collective-permute-start(f32[7,64]{1,0:T(8,128)S(1)} %get-tuple-element.331), channel_id=1, source_target_pairs={{4,0},{8,4},{12,8},{16,12},{20,16},{24,20},{28,24},{32,28},{36,32}... | collective-permute-start | bytes 5384 | tf_op jit(solution)/shard_map/ppermute | solution.py:27
  17.1 28.1 %while.24 = (s32[]{:T(128)}, f32[2448,256]{1,0:T(8,128)}, f32[5,128,7]{1,2,0:T(8,128)S(1)}, s32[]{:T(128)}, s32[]{:T(128)}) while((s32[]{:T(128)}, f32[2448,256]{1,0:T(8,128)}, f32[5,128,7]{1,2,0:T(8,128)S(1)}, s32[]{:T(128)}, s32[]{:T(128)}) %tuple.143), condition=%wide.region_1.2_spmd.clone, body=%wide.region_0.1_spmd.clone.sunk | while | flops 965456192 | bytes 10168011 | solution.py:269
  21.8 5.5 convolution_add_fusion.2
  27.8 5.5 convolution_add_fusion.2
  33.8 5.5 convolution_add_fusion.2
  39.7 5.5 convolution_add_fusion.2
  47.8 5.1 collective-permute-start.3
  53.0 5.8 %collective-permute-done.2 = f32[3,2,68,256]{3,2,1,0:T(8,128)S(1)} collective-permute-done((f32[3,2,68,256]{3,2,1,0:T(8,128)S(1)}, f32[3,2,68,256]{3,2,1,0:T(8,128)S(1)}, u32[]{:S(2)}, u32[]{:S(2)}) %collective-permute-start.2) | collective-permute-done | bytes 417824 | tf_op jit(solution)/shard_map/ppermute | solution.py:25
  75.5 4.8 all-to-all-start
  83.6 8.9 %all-to-all-done = f32[4,1,98304]{2,1,0:T(1,128)S(1)} async-done(((f32[4,1,98304]{2,1,0:T(1,128)}), f32[4,1,98304]{2,1,0:T(1,128)S(1)}, u32[]{:S(2)}, u32[]{:S(2)}) %all-to-all-start) | async-done | bytes 1572896 | tf_op jit(solution)/shard_map/all_to_all | solution.py:297
  93.0 6.3 %reduce.20 = f32[4,98304]{1,0:T(4,128)} reduce(f32[4,1,98304]{2,1,0:T(1,128)S(1)} %all-to-all-done, f32[]{:T(128)} %broadcast.2020), dimensions={1}, to_apply=%all_to_all.48.reduce_sub_computation | reduce | bytes 3145732 | tf_op jit(solution)/shard_map/all_to_all | solution.py:297
  120.5 20.7 %scatter.20 = f32[3,8,256,64]{3,1,0,2:T(8,128)S(1)} dynamic-update-slice(f32[3,8,256,64]{3,1,0,2:T(8,128)S(1)} %copy.199, f32[3,8,256,1]{3,1,0,2:T(8,128)} %copy.200, s32[]{:T(128)} %constant.601.clone.1, s32[]{:T(128)} %constant.601.clone.1, s32[]{:T(128)} %constant.601.clone.1, s32[]{:T(128)} %constant.601.clone.1) | dynamic-update-slice | bytes 49156 | tf_op jit(solution)/shard_map/scatter | solution.py:119
  141.3 72.1 %scatter.21 = f32[3,8,256,64]{3,1,0,2:T(8,128)S(1)} dynamic-update-slice(f32[3,8,256,64]{3,1,0,2:T(8,128)S(1)} %scatter.20, f32[3,8,256,1]{3,1,0,2:T(8,128)} %copy.201, s32[]{:T(128)} %constant.601.clone.1, s32[]{:T(128)} %constant.601.clone.1, s32[]{:T(128)} %constant.601.clone.1, s32[]{:T(128)} %constant.603.clone.1) | dynamic-update-slice | bytes 49156 | tf_op jit(solution)/shard_map/scatter | solution.py:120
  216.3 11.0 %all-to-all-start.1 = ((f32[64,1,6144]{2,1,0:T(1,128)}), f32[64,1,6144]{2,1,0:T(1,128)S(1)}, u32[]{:S(2)}, u32[]{:S(2)}) async-start(f32[64,1,6144]{2,1,0:T(1,128)} %reshape.1397), calls=%async_computation.1 | async-start | bytes 3145728 | tf_op jit(solution)/shard_map/all_to_all | solution.py:308
  231.3 3.9 broadcast_multiply_fusion.3
  236.7 4.1 fusion.79
  240.8 26.0 %all-to-all-done.1 = f32[64,1,6144]{2,1,0:T(1,128)S(1)} async-done(((f32[64,1,6144]{2,1,0:T(1,128)}), f32[64,1,6144]{2,1,0:T(1,128)S(1)}, u32[]{:S(2)}, u32[]{:S(2)}) %all-to-all-start.1) | async-done | bytes 1572896 | tf_op jit(solution)/shard_map/all_to_all | solution.py:308
  266.8 5.9 %reduce.21 = f32[64,6144]{1,0:T(8,128)} reduce(f32[64,1,6144]{2,1,0:T(1,128)S(1)} %all-to-all-done.1, f32[]{:T(128)} %broadcast.2020), dimensions={1}, to_apply=%all_to_all.51.reduce_sub_computation | reduce | bytes 3145732 | tf_op jit(solution)/shard_map/all_to_all | solution.py:308
  277.1 7.3 %reshape.1376 = f32[3,512,4,2,32]{4,3,1,2,0:T(2,128)} reshape(f32[3,64,8,4,64]{4,2,1,3,0:T(8,128)} %copy.203) | data formatting | bytes 3145728 | tf_op jit(solution)/shard_map/reshape | solution.py:61
  284.3 43.0 %fusion.92 = f32[3,512,4,2,32]{1,4,3,2,0:T(8,128)S(1)} fusion(f32[1,512,2,512]{3,1,2,0:T(8,128)S(1)} %copy-done.4, f32[1,512,2,512]{3,1,2,0:T(8,128)} %get-tuple-element.308, f32[3,512,4,2,32,1]{4,3,1,2,0,5:T(2,128)} %bitcast.212), kind=kOutput, calls=%fused_computation.147 | convolution fusion | flops 4832886784 | bytes 7340032 | tf_op jit(solution)/shard_map/qkrz,bzxrm->bkxqm/dot_general | solution.py:305
  337.1 8.5 %bitcast_multiply_fusion.1 = f32[3,4,32,2,512]{4,2,3,1,0:T(8,128)} fusion(f32[3,512,4,2,32,1]{1,4,3,5,2,0:T(8,128)} %bitcast.227, f32[1,512,2,512]{3,1,2,0:T(8,128)} %get-tuple-element.309, f32[1,512,2,512]{3,1,2,0:T(8,128)S(1)} %copy-done.3), kind=kOutput, calls=%fused_computation.141 | convolution fusion | flops 4833280000 | bytes 7340032 | tf_op jit(solution)/shard_map/qkrz,bzxrm->bkxqm/dot_general | solution.py:316
  352.5 46.1 %all_to_all.66 = f32[64,1,6144]{2,1,0:T(1,128)S(1)} all-to-all(f32[64,1,6144]{2,1,0:T(1,128)} %reshape.1399), channel_id=1, replica_groups=mesh['gz'=64,'gx'=4] {'gz'}, dimensions={0} | all-to-all | bytes 3145728 | tf_op jit(solution)/shard_map/all_to_all | solution.py:318
  398.6 5.9 %reduce.22 = f32[64,6144]{1,0:T(8,128)} reduce(f32[64,1,6144]{2,1,0:T(1,128)S(1)} %all_to_all.66, f32[]{:T(128)} %broadcast.2020), dimensions={1}, to_apply=%all_to_all.54.reduce_sub_computation | reduce | bytes 3145732 | tf_op jit(solution)/shard_map/all_to_all | solution.py:318
  419.8 11.8 %scatter.26 = f32[3,8,256,64]{3,1,2,0:T(8,128)S(1)} dynamic-update-slice(f32[3,8,256,64]{3,1,2,0:T(8,128)S(1)} %bitcast.211, f32[3,8,256,1]{3,1,2,0:T(8,128)} %copy.221, s32[]{:T(128)} %constant.601.clone.1, s32[]{:T(128)} %constant.601.clone.1, s32[]{:T(128)} %constant.601.clone.1, s32[]{:T(128)} %constant.601.clone.1) | dynamic-update-slice | bytes 49156 | tf_op jit(solution)/shard_map/scatter | solution.py:143
  433.9 63.6 %scatter.29 = f32[3,8,256,64]{3,1,2,0:T(8,128)S(1)} dynamic-update-slice(f32[3,8,256,64]{3,1,2,0:T(8,128)S(1)} %scatter.26, f32[3,8,256,1]{3,1,2,0:T(8,128)} %copy.222, s32[]{:T(128)} %constant.601.clone.1, s32[]{:T(128)} %constant.601.clone.1, s32[]{:T(128)} %constant.601.clone.1, s32[]{:T(128)} %constant.603.clone.1) | dynamic-update-slice | bytes 49156 | tf_op jit(solution)/shard_map/scatter | solution.py:144
  499.7 5.5 bitcast_multiply_fusion
  510.4 5.1 all-to-all-start.3
  516.8 18.8 %all-to-all-done.3 = f32[4,1,98304]{2,1,0:T(1,128)S(1)} async-done(((f32[4,1,98304]{2,1,0:T(1,128)}), f32[4,1,98304]{2,1,0:T(1,128)S(1)}, u32[]{:S(2)}, u32[]{:S(2)}) %all-to-all-start.3) | async-done | bytes 1572896 | tf_op jit(solution)/shard_map/all_to_all | solution.py:325
  535.6 6.3 %reduce.23 = f32[4,98304]{1,0:T(4,128)} reduce(f32[4,1,98304]{2,1,0:T(1,128)S(1)} %all-to-all-done.3, f32[]{:T(128)} %broadcast.2020), dimensions={1}, to_apply=%all_to_all.58.reduce_sub_computation | reduce | bytes 3145732 | tf_op jit(solution)/shard_map/all_to_all | solution.py:325
  541.9 4.5 reshape.1402
  546.4 5.6 copy.269
  561.4 5.3 collective-permute-done.7
  (237 shorter events, 129.0 us)
Async XLA Ops:
  8.1 8.8 %collective-permute-start = (f32[7,64]{1,0:T(8,128)S(1)}, f32[7,64]{1,0:T(8,128)S(1)}, u32[]{:S(2)}, u32[]{:S(2)}) collective-permute-start(f32[7,64]{1,0:T(8,128)S(1)} %get-tuple-element.330), channel_id=1, source_target_pairs={{0,4},{4,8},{8,12},{12,16},{16,20},{20,24},{24,28},{28,32},{32,36}... | collective-permute-start | bytes 5384 | tf_op jit(solution)/shard_map/ppermute | solution.py:25
  8.1 8.9 %collective-permute-start.1 = (f32[7,64]{1,0:T(8,128)S(1)}, f32[7,64]{1,0:T(8,128)S(1)}, u32[]{:S(2)}, u32[]{:S(2)}) collective-permute-start(f32[7,64]{1,0:T(8,128)S(1)} %get-tuple-element.331), channel_id=1, source_target_pairs={{4,0},{8,4},{12,8},{16,12},{20,16},{24,20},{28,24},{32,28},{36,32}... | collective-permute-start | bytes 5384 | tf_op jit(solution)/shard_map/ppermute | solution.py:27
  47.7 11.1 %collective-permute-start.2 = (f32[3,2,68,256]{3,2,1,0:T(8,128)S(1)}, f32[3,2,68,256]{3,2,1,0:T(8,128)S(1)}, u32[]{:S(2)}, u32[]{:S(2)}) collective-permute-start(f32[3,2,68,256]{3,2,1,0:T(8,128)S(1)} %get-tuple-element.275), channel_id=1, source_target_pairs={{0,4},{4,8},{8,12},{12,16},{16,20},{20,24},{24,28},{28,32},{32,36}... | collective-permute-start | bytes 1253384 | tf_op jit(solution)/shard_map/ppermute | solution.py:25
  47.8 11.1 %collective-permute-start.3 = (f32[3,2,68,256]{3,2,1,0:T(8,128)S(1)}, f32[3,2,68,256]{3,2,1,0:T(8,128)S(1)}, u32[]{:S(2)}, u32[]{:S(2)}) collective-permute-start(f32[3,2,68,256]{3,2,1,0:T(8,128)S(1)} %get-tuple-element.274), channel_id=1, source_target_pairs={{4,0},{8,4},{12,8},{16,12},{20,16},{24,20},{28,24},{32,28},{36,32}... | collective-permute-start | bytes 1253384 | tf_op jit(solution)/shard_map/ppermute | solution.py:27
  59.1 4.2 collective-permute-start.4
  60.7 4.4 copy-start.13
  60.9 4.2 collective-permute-start.5
  65.4 1.2 copy-start.1
  75.5 17.0 %all-to-all-start = ((f32[4,1,98304]{2,1,0:T(1,128)}), f32[4,1,98304]{2,1,0:T(1,128)S(1)}, u32[]{:S(2)}, u32[]{:S(2)}) async-start(f32[4,1,98304]{2,1,0:T(1,128)} %reshape.1395), calls=%async_computation | async-start | bytes 3145728 | tf_op jit(solution)/shard_map/all_to_all | solution.py:297
  105.9 3.6 copy-start.11
  105.9 3.6 copy-start.12
  112.1 1.1 copy-start.6
  216.3 50.5 %all-to-all-start.1 = ((f32[64,1,6144]{2,1,0:T(1,128)}), f32[64,1,6144]{2,1,0:T(1,128)S(1)}, u32[]{:S(2)}, u32[]{:S(2)}) async-start(f32[64,1,6144]{2,1,0:T(1,128)} %reshape.1397), calls=%async_computation.1 | async-start | bytes 3145728 | tf_op jit(solution)/shard_map/all_to_all | solution.py:308
  277.1 7.3 %copy-start.4 = (f32[1,512,2,512]{3,1,2,0:T(8,128)S(1)}, f32[1,512,2,512]{3,1,2,0:T(8,128)}, u32[]{:S(2)}) copy-start(f32[1,512,2,512]{3,1,2,0:T(8,128)} %get-tuple-element.277) | copy-start | bytes 6291460
  327.3 2.4 copy-start.7
  331.2 5.9 %copy-start.3 = (f32[1,512,2,512]{3,1,2,0:T(8,128)S(1)}, f32[1,512,2,512]{3,1,2,0:T(8,128)}, u32[]{:S(2)}) copy-start(f32[1,512,2,512]{3,1,2,0:T(8,128)} %get-tuple-element.276) | copy-start | bytes 6291460
  331.5 1.1 copy-start.5
  510.4 5.1 copy-start.2
  510.4 25.2 %all-to-all-start.3 = ((f32[4,1,98304]{2,1,0:T(1,128)}), f32[4,1,98304]{2,1,0:T(1,128)S(1)}, u32[]{:S(2)}, u32[]{:S(2)}) async-start(f32[4,1,98304]{2,1,0:T(1,128)} %reshape.1401), calls=%async_computation.3 | async-start | bytes 3145728 | tf_op jit(solution)/shard_map/all_to_all | solution.py:325
  558.1 14.1 %copy-start = (f32[3,8,64,256]{3,2,1,0:T(8,128)}, f32[3,8,64,256]{3,2,1,0:T(8,128)S(1)}, u32[]{:S(2)}) copy-start(f32[3,8,64,256]{3,2,1,0:T(8,128)S(1)} %fusion.125) | copy-start | bytes 4718596
  558.1 3.3 collective-permute-start.6
  558.2 8.5 %collective-permute-start.7 = (f32[3,1,64,256]{3,2,1,0:T(8,128)S(1)}, f32[3,1,64,256]{3,2,1,0:T(8,128)S(1)}, u32[]{:S(2)}, u32[]{:S(2)}) collective-permute-start(f32[3,1,64,256]{3,2,1,0:T(8,128)S(1)} %get-tuple-element.298), channel_id=1, source_target_pairs={{0,4},{4,8},{8,12},{12,16},{16,20},{20,24},{24,28},{28,32},{32,36}... | collective-permute-start | bytes 589832 | tf_op jit(solution)/shard_map/ppermute | solution.py:25
  566.8 4.0 collective-permute-start.8
  568.3 3.9 copy-start.8
  568.3 3.9 copy-start.9
  568.3 3.9 copy-start.10
  568.3 3.9 collective-permute-start.9
where the time goes:
time: 586 us; the launch traced here: 576 us
  local copies, waits for them, and re-layouts  266 us (45%)
  matrix products  91.5 us (16%)
  waiting for transfers between devices  74.9 us (13%)
  other arithmetic  53.1 us (9%)
  blocking collectives  46.1 us (8%)
  starting transfers between devices  38.6 us (7%)
    scatter x1, local copies, waits for them, and re-layouts, reslot(): values.at[..., mode_count].set(jnp.where(first_pencil, new_imag, imag_part))  72.1 us
    scatter x2, local copies, waits for them, and re-layouts, unslot(): values.at[..., mode_count].set(jnp.where(first_pencil, new_imag, imag_part))  65.8 us
    all_to_all x1, blocking collectives, on_device(): lax.all_to_all(physical, 'gz', split_axis=1, concat_axis=2, tiled=True)  46.1 us
    dot_general x1, matrix products, on_device(): jnp.einsum('qkrz,bzxrm->bkxqm', ahead_z_table, split_pairs(lax.all_to_all...  43 us
    unnamed x48, local copies, waits for them, and re-layouts  35.5 us
    all_to_all x1, waiting for transfers between devices, on_device(): lax.all_to_all(spectral, 'gz', split_axis=2, concat_axis=1, tiled=True)  26 us
    dot_general x5, matrix products, deposit(): lax.dot_general(spread, weight_y, (((0,), (0,)), ((), ())), precision=hig...  25.7 us
    scatter x1, local copies, waits for them, and re-layouts, reslot(): values = values.at[..., 0].set(jnp.where(first_pencil, new_real, real_part))  20.7 us
  transfers between devices with their start and end apart: 13, of which 12 were waited for; matrix products, arithmetic and copies ran while one was open for 3% of the time, Pallas kernels for 0%

commit v1 on v0

v1 whole, which is shorter than its diff:
```python
import functools
import math

import jax
import jax.numpy as jnp
import ml_dtypes
import numpy as np
from jax import lax
from jax.experimental import pallas as pl
from jax.experimental.pallas import tpu as pltpu
from jax.sharding import PartitionSpec as P

MESH = pl.DeviceIdType.MESH
F32 = jnp.float32
BF16 = jnp.bfloat16
PENCILS = 4
MODES = 32
PLANES = 8
KXS = 4


def halves(table):
    high = table.astype(ml_dtypes.bfloat16)
    low = (table - high.astype(np.float64)).astype(ml_dtypes.bfloat16)
    return np.stack([high, low])


def real_form(angle):
    cosine, sine = np.cos(angle), np.sin(angle)
    return np.stack([np.stack([cosine, sine], -1), np.stack([-sine, cosine], -1)], -2)


def kx_of(slabs):
    base = 2 * np.arange(slabs)
    rows = np.stack([base, base + 1, -base, -base - 1], 1) % (4 * slabs)
    rows[0, 2] = 2 * slabs
    return rows


def tables(slabs):
    nx, nz, ny = 4 * slabs, 8 * slabs, 2 * MODES * PENCILS
    rows = 8 * slabs
    two_pi = 2.0 * np.pi
    y = np.arange(ny)
    ahead_y, back_y = [], []
    for r in range(4):
        block = (np.arange(4) - r) % 4
        ky = (block[:, None] * MODES + np.arange(MODES)[None, :]).reshape(-1)
        angle = two_pi * (y[:, None] * ky[None, :] % ny) / ny
        cosine, sine = np.cos(angle), -np.sin(angle)
        sine = np.where(ky[None, :] == 0, (1.0 - 2.0 * (y % 2))[:, None], sine)
        table = np.concatenate([cosine, sine], 1)
        weight = np.where(ky == 0, 1.0, 2.0) / ny
        ahead_y.append(halves(table))
        back_y.append(halves(table.T * np.concatenate([weight, weight])[:, None]))
    kx = kx_of(slabs).reshape(-1)
    x = np.arange(nx)
    form = real_form(two_pi * (kx[:, None] * x[None, :] % nx) / nx)
    form = form.reshape(nx, PENCILS, nx // PENCILS, 2, 2).transpose(0, 3, 1, 4, 2)
    table_x = form.reshape(rows, rows)
    k1 = np.arange(slabs)
    form = real_form(two_pi * (k1[:, None] * k1[None, :] % slabs) / slabs)
    same = np.eye(KXS)
    table_1 = np.einsum("ksoi,ab->okasbi", form, same).reshape(rows, rows)
    k2 = np.arange(PLANES)
    form = real_form(two_pi * (k2[:, None] * k2[None, :] % PLANES) / PLANES)
    table_2 = np.einsum("kpoi,ab->ipaokb", form, np.eye(MODES)).reshape(2 * PLANES * MODES, -1)
    angle = two_pi * (k1[:, None] * k2[None, :]) / nz
    angle = np.repeat(np.repeat(angle, KXS, 0), MODES, 1)
    twiddle = np.stack([np.cos(angle), np.sin(angle)]).astype(np.float32)
    return (
        np.stack(ahead_y), np.stack(back_y), halves(table_x), halves(table_x.T / nx),
        halves(table_1), halves(table_1.T / nz), halves(table_2), halves(table_2.T), twiddle,
    )


def split(values):
    high = values.astype(BF16)
    return high, (values - high.astype(F32)).astype(BF16)


def dot(a, b):
    return jnp.dot(a, b, preferred_element_type=F32)


def table_times(table, values):
    high, low = split(values)
    return dot(table[0], high) + (dot(table[0], low) + dot(table[1], high))


def times_table(values, table):
    high, low = split(values)
    return dot(high, table[0]) + (dot(low, table[0]) + dot(high, table[1]))


def spectral_kernel(
    slabs, vort, ahead_y, back_y, ahead_x, back_x, ahead_1, back_1, ahead_2, back_2, twiddle,
    vel, ys, xr, xo, zr, spec, zo, xr2, xo2, yr, send_sem, recv_sem, own_sem,
):
    me_z, me_x = lax.axis_index("gz"), lax.axis_index("gx")
    nx = 4 * slabs
    xl = nx // PENCILS
    rows = 8 * slabs
    half = 4 * slabs
    part = 2 * xl
    lanes = PLANES * MODES

    barrier = pltpu.get_barrier_semaphore()

    def greet(i, carry):
        pl.semaphore_signal(barrier, inc=1, device_id={"gz": lax.rem(me_z + i, slabs)}, device_id_type=MESH)
        return carry

    lax.fori_loop(1, slabs, greet, 0)
    for i in range(1, PENCILS):
        pl.semaphore_signal(barrier, inc=1, device_id={"gx": lax.rem(me_x + i, PENCILS)}, device_id_type=MESH)
    pl.semaphore_wait(barrier, slabs - 1 + PENCILS - 1)

    def own_copy(src, dst, c, stage, width, index):
        at = pl.ds(pl.multiple_of(index * width, 8), width)
        return pltpu.make_async_copy(src.at[c, at], dst.at[c, at], own_sem.at[stage, c])

    def send_gx(src, dst, c, stage):
        mine = pl.ds(pl.multiple_of(me_x * part, 8), part)
        for i in (2, 1, 3):
            other = lax.rem(me_x + i, PENCILS)
            pltpu.make_async_remote_copy(
                src_ref=src.at[c, pl.ds(pl.multiple_of(other * part, 8), part)],
                dst_ref=dst.at[c, mine],
                send_sem=send_sem.at[stage, c],
                recv_sem=recv_sem.at[stage, c],
                device_id={"gx": other},
                device_id_type=MESH,
            ).start()
        own_copy(src, dst, c, stage, part, me_x).start()

    def send_gz(src, dst, c, stage):
        mine = pl.ds(pl.multiple_of(me_z * 8, 8), 8)

        def one(i, carry):
            step = lax.div(i + 1, 2)
            step = step + lax.rem(i + 1, 2) * (slabs - 2 * step)
            other = lax.rem(me_z + step, slabs)
            pltpu.make_async_remote_copy(
                src_ref=src.at[c, pl.ds(pl.multiple_of(other * 8, 8), 8)],
                dst_ref=dst.at[c, mine],
                send_sem=send_sem.at[stage, c],
                recv_sem=recv_sem.at[stage, c],
                device_id={"gz": other},
                device_id_type=MESH,
            ).start()
            return carry

        lax.fori_loop(1, slabs, one, 0)
        own_copy(src, dst, c, stage, 8, me_z).start()

    def remote_rows(stage):
        return part * (PENCILS - 1) if stage in (0, 3) else 8 * (slabs - 1)

    def arrive(src, dst, c, stage):
        window = dst.at[c, pl.ds(0, remote_rows(stage))]
        pltpu.make_async_copy(window, window, recv_sem.at[stage, c]).wait()
        width, index = (part, me_x) if stage in (0, 3) else (8, me_z)
        own_copy(src, dst, c, stage, width, index).wait()

    def sent(src, c, stage):
        window = src.at[c, pl.ds(0, remote_rows(stage))]
        pltpu.make_async_copy(window, window, send_sem.at[stage, c]).wait()

    for c in range(3):
        spread = []
        for r in range(4):
            cells = jnp.concatenate([vort[c, r], vort[c, r + 4]], axis=0)
            spread.append(times_table(cells, ahead_y[r]))
        spot = lax.broadcasted_iota(jnp.int32, (part, 128), 1) // MODES
        for b in range(PENCILS):
            for p in range(2):
                picked = spread[0][:, p * 128:(p + 1) * 128]
                for r in range(1, 4):
                    picked = jnp.where(spot == (b + r) % 4, spread[r][:, p * 128:(p + 1) * 128], picked)
                if b:
                    picked = pltpu.roll(picked, 128 - MODES * b, 1)
                at = b * part + p * xl
                ys[c, at:at + xl, 0:128] = picked[:xl]
                ys[c, at:at + xl, 128:256] = picked[xl:]
        send_gx(ys, xr, c, 0)
    for c in range(3):
        arrive(ys, xr, c, 0)
        xo[c] = table_times(ahead_x, xr[c])
        send_gz(xo, zr, c, 1)
    cos_t, sin_t = twiddle[0], twiddle[1]
    for c in range(3):
        arrive(xo, zr, c, 1)
        mixed = table_times(ahead_1, zr[c])
        real, imag = mixed[:half], mixed[half:]
        turned = jnp.concatenate([real * cos_t + imag * sin_t, imag * cos_t - real * sin_t], axis=1)
        spec[c] = times_table(turned, ahead_2)
    row = lax.broadcasted_iota(jnp.int32, (half, lanes), 0)
    lane = lax.broadcasted_iota(jnp.int32, (half, lanes), 1)
    slot = row % KXS
    k1 = row // KXS
    kz = k1 + slabs * (lane // MODES)
    mode = lane % MODES
    base = 2 * me_z
    kx = base + slot % 2
    kx = jnp.where(slot >= 2, -kx, kx)
    kx = jnp.where((slot == 2) & (me_z == 0), nx // 2, kx)
    nz = 8 * slabs
    ky = me_x * MODES + mode
    wave_z = jnp.where(kz < nz // 2, kz, kz - nz).astype(F32) * (2.0 * math.pi / nz)
    wave_x = kx.astype(F32) * (2.0 * math.pi / nx)
    wave_y = ky.astype(F32) * (2.0 * math.pi / (2 * MODES * PENCILS))
    flat_sq = wave_z * wave_z + wave_x * wave_x
    packed = ky == 0
    anchor = (kz == 0) & (kx == 0) & packed
    wave_sq = flat_sq + wave_y * wave_y
    inverse = jnp.where(anchor, 0.0, 1.0 / jnp.where(anchor, 1.0, wave_sq))
    odd_inverse = 1.0 / (flat_sq + math.pi * math.pi)
    even = jnp.where(packed, 0.5 * (inverse + odd_inverse), inverse)
    cross = jnp.where(packed, 0.5 * (inverse - odd_inverse), 0.0)
    wave_z = jnp.where(kz == nz // 2, 0.0, wave_z)
    wave_x = jnp.where((kx == nx // 2), 0.0, wave_x)
    to = lax.broadcasted_iota(jnp.int32, (half, half), 0)
    fro = lax.broadcasted_iota(jnp.int32, (half, half), 1)
    to_slot = to % KXS
    mirror_slot = jnp.where(
        (me_z == 0), jnp.where(to_slot % 2 == 0, to_slot, 4 - to_slot), (to_slot + 2) % 4
    )
    mirror_row = ((slabs - to // KXS) % slabs) * KXS + mirror_slot
    row_swap = jnp.where(fro == mirror_row, 1.0, 0.0).astype(BF16)
    fro = lax.broadcasted_iota(jnp.int32, (2 * lanes, 2 * lanes), 0)
    to = lax.broadcasted_iota(jnp.int32, (2 * lanes, 2 * lanes), 1)
    mirror_lane = (to // lanes) * lanes + (PLANES - 1 - (to % lanes) // MODES) * MODES
    sign = jnp.where(to < lanes, 1.0, -1.0)
    lane_swap = jnp.where((fro == mirror_lane) & (to % MODES == 0), sign, 0.0).astype(BF16)
    stream = []
    for c in range(3):
        modes = spec[c]
        high, low = split(modes)
        swapped = dot(row_swap, high) + dot(row_swap, low)
        high, low = split(swapped)
        swapped = dot(high, lane_swap) + dot(low, lane_swap)
        pair = []
        for p in range(2):
            mirror = swapped[:, p * lanes:(p + 1) * lanes]
            mirror = jnp.where(k1 == 0, jnp.concatenate([mirror[:, lanes - MODES:], mirror[:, :lanes - MODES]], axis=1), mirror)
            pair.append(even * modes[:, p * lanes:(p + 1) * lanes] + cross * mirror)
        stream.append(pair)

    def curl(c, p):
        if c == 0:
            return wave_x * stream[2][p] - wave_y * stream[1][p]
        if c == 1:
            return wave_y * stream[0][p] - wave_z * stream[2][p]
        return wave_z * stream[1][p] - wave_x * stream[0][p]

    for c in range(3):
        turned = times_table(jnp.concatenate([-curl(c, 1), curl(c, 0)], axis=1), back_2)
        real, imag = turned[:, :lanes], turned[:, lanes:]
        mixed = jnp.concatenate([real * cos_t - imag * sin_t, imag * cos_t + real * sin_t], axis=0)
        zo[c] = table_times(back_1, mixed)
        send_gz(zo, xr2, c, 2)
    for c in range(3):
        arrive(zo, xr2, c, 2)
        xo2[c] = table_times(back_x, xr2[c])
        send_gx(xo2, yr, c, 3)
    spot = lax.broadcasted_iota(jnp.int32, (xl, 128), 1) // MODES
    for c in range(3):
        arrive(xo2, yr, c, 3)
        rolled = {}
        for zh in range(2):
            for b in range(PENCILS):
                for p in range(2):
                    at = b * part + p * xl
                    tile = yr[c, at:at + xl, zh * 128:(zh + 1) * 128]
                    rolled[zh, b, p] = pltpu.roll(tile, MODES * b, 1) if b else tile
        for r in range(4):
            sides = []
            for zh in range(2):
                both = []
                for p in range(2):
                    picked = rolled[zh, 0, p]
                    for b in range(1, 4):
                        picked = jnp.where(spot == (b + r) % 4, rolled[zh, b, p], picked)
                    both.append(picked)
                sides.append(jnp.concatenate(both, axis=1))
            cells = times_table(jnp.concatenate(sides, axis=0), back_y[r])
            vel[c, r] = cells[:xl]
            vel[c, r + 4] = cells[xl:]
    for c in range(3):
        sent(ys, c, 0)
        sent(xo, c, 1)
        sent(zo, c, 2)
        sent(xo2, c, 3)


def spectral(vort, slabs):
    consts = [jnp.asarray(t) for t in tables(slabs)]
    rows = 8 * slabs
    lanes = PLANES * MODES
    wide = pltpu.VMEM((3, rows, lanes), F32)
    return pl.pallas_call(
        functools.partial(spectral_kernel, slabs),
        out_shape=jax.ShapeDtypeStruct(vort.shape, F32),
        in_specs=[pl.BlockSpec(memory_space=pltpu.VMEM)] * (1 + len(consts)),
        out_specs=pl.BlockSpec(memory_space=pltpu.VMEM),
        scratch_shapes=[
            wide, wide, wide, wide,
            pltpu.VMEM((3, 4 * slabs, 2 * lanes), F32),
            wide, wide, wide, wide,
            pltpu.SemaphoreType.DMA((4, 3)),
            pltpu.SemaphoreType.DMA((4, 3)),
            pltpu.SemaphoreType.DMA((4, 3)),
        ],
        compiler_params=pltpu.CompilerParams(
            collective_id=0, has_side_effects=True, vmem_limit_bytes=56 * 1024 * 1024
        ),
    )(vort, *consts)


NY = 256
PART = 512
MIG = 64
time_step = 0.25


def padded_2(cells, sides, width):
    for axis, dim in sides:
        count = lax.axis_size(axis)
        head = lax.slice_in_dim(cells, 0, width, axis=dim)
        tail = lax.slice_in_dim(cells, cells.shape[dim] - width, cells.shape[dim], axis=dim)
        cells = jnp.concatenate(
            [
                lax.ppermute(tail, axis, [(i, (i + 1) % count) for i in range(count)]),
                cells,
                lax.ppermute(head, axis, [((i + 1) % count, i) for i in range(count)]),
            ],
            axis=dim,
        )
    return cells


def kernel_weight(distance):
    radius = jnp.abs(distance)
    near_part = 1.0 - 2.5 * radius * radius + 1.5 * radius * radius * radius
    far_part = 0.5 * (2.0 - radius) * (2.0 - radius) * (1.0 - radius)
    return jnp.where(radius < 1.0, near_part, jnp.where(radius < 2.0, far_part, 0.0))


def on_device(strength, offsets, cell_index, migrate_count, ambient):
    slab_planes = ambient.shape[1]
    pencil_cols = ambient.shape[2]
    slab_count = lax.axis_size("gz")
    up_count = migrate_count[0, 0, 0]
    down_count = migrate_count[0, 0, 1]
    slot_index = jnp.arange(PART, dtype=jnp.int32)
    packet = jnp.concatenate([strength, offsets, cell_index.astype(jnp.float32)[None, :]], axis=0)
    is_strength = (jnp.arange(7) < 3)[:, None]
    head_live = slot_index[:MIG] < up_count
    upward = jnp.where(is_strength & ~head_live[None, :], 0.0, packet[:, :MIG])
    downward = lax.dynamic_slice_in_dim(packet, up_count, MIG, axis=1)
    down_live = jnp.arange(MIG, dtype=jnp.int32) < down_count
    downward = jnp.where(is_strength & ~down_live[None, :], 0.0, downward)
    outgoing = jnp.concatenate([downward, upward], axis=1)
    extended = padded_2(outgoing, (("gz", 1),), MIG)
    arrived = jnp.concatenate([extended[:, :MIG], extended[:, 3 * MIG :]], axis=1)
    staying = slot_index >= up_count + down_count
    retained = jnp.where(is_strength & ~staying[None, :], 0.0, packet)
    particles = jnp.concatenate([retained, arrived], axis=1)
    particle_total = particles.shape[1]
    block_rows = math.gcd(particle_total, 256)
    row_blocks = particles.T.reshape(particle_total // block_rows, block_rows, 7)
    planes = jnp.arange(slab_planes + 4, dtype=jnp.int32) - 2
    columns = jnp.arange(pencil_cols + 4, dtype=jnp.int32) - 2
    lateral = jnp.arange(NY, dtype=jnp.int32)

    def deposit(deposited, row_group):
        cell_ids = row_group[:, 6].astype(jnp.int32)
        z_cell = cell_ids // (pencil_cols * NY)
        x_cell = cell_ids // NY % pencil_cols
        y_cell = cell_ids % NY
        weight_z = kernel_weight(
            (planes[None, :] - z_cell[:, None]).astype(jnp.float32) - row_group[:, 3:4]
        )
        weight_x = kernel_weight(
            (columns[None, :] - x_cell[:, None]).astype(jnp.float32) - row_group[:, 4:5]
        )
        y_offset = (lateral[None, :] - y_cell[:, None] + NY // 2) % NY - NY // 2
        weight_y = kernel_weight(y_offset.astype(jnp.float32) - row_group[:, 5:6])
        spread = (
            row_group[:, 0:3, None, None] * weight_z[:, None, :, None] * weight_x[:, None, None, :]
        )
        spread = spread.reshape(block_rows, -1)
        added = lax.dot_general(
            spread,
            weight_y,
            (((0,), (0,)), ((), ())),
            precision=lax.Precision.HIGHEST,
            preferred_element_type=jnp.float32,
        )
        return (deposited + added, None)

    start_mesh = jnp.zeros((3 * (slab_planes + 4) * (pencil_cols + 4), NY), jnp.float32)
    deposited, _ = lax.scan(deposit, start_mesh, row_blocks)
    deposited = deposited.reshape(3, slab_planes + 4, pencil_cols + 4, NY)
    plane_rim = jnp.concatenate([deposited[:, :2], deposited[:, slab_planes + 2 :]], axis=1)
    plane_rim = padded_2(plane_rim, (("gz", 1),), 2)
    interior = deposited[:, 2 : slab_planes + 2]
    interior = (
        interior.at[:, :2].add(plane_rim[:, :2]).at[:, slab_planes - 2 :].add(plane_rim[:, 6:])
    )
    column_rim = jnp.concatenate([interior[:, :, :2], interior[:, :, pencil_cols + 2 :]], axis=2)
    column_rim = padded_2(column_rim, (("gx", 2),), 2)
    interior = interior[:, :, 2 : pencil_cols + 2]
    interior = (
        interior.at[:, :, :2]
        .add(column_rim[:, :, :2])
        .at[:, :, pencil_cols - 2 :]
        .add(column_rim[:, :, 6:])
    )
    vorticity_mesh = ambient + interior
    velocity = spectral(vorticity_mesh, slab_count)
    padded = padded_2(velocity, (("gz", 1), ("gx", 2)), 1)
    along_z = (padded[:, 2:, 1:-1] - padded[:, :-2, 1:-1]) * 0.5
    along_x = (padded[:, 1:-1, 2:] - padded[:, 1:-1, :-2]) * 0.5
    along_y = (jnp.roll(velocity, -1, axis=3) - jnp.roll(velocity, 1, axis=3)) * 0.5
    stretch = (
        vorticity_mesh[0] * along_z + vorticity_mesh[1] * along_x + vorticity_mesh[2] * along_y
    )
    return (velocity, vorticity_mesh + time_step * stretch)


def solution(mesh):
    placed = (
        P(None, ("gz", "gx")),
        P(None, ("gz", "gx")),
        P(("gz", "gx")),
        P("gz", "gx", None),
        P(None, "gz", "gx", None),
    )
    return jax.shard_map(
        on_device,
        mesh=mesh,
        in_specs=placed,
        out_specs=(P(None, "gz", "gx", None), P(None, "gz", "gx", None)),
        check_vma=False,
    )
```

time: 586 us -> 199 us (0.34); the launches traced: 576 us -> 197 us
  local copies, waits for them, and re-layouts: 266 us -> 8.7 us
  Pallas kernels: 0 us -> 110 us
  matrix products: 91.5 us -> 25.7 us
  waiting for transfers between devices: 74.9 us -> 20.9 us
  blocking collectives: 46.1 us -> 0 us
  other arithmetic: 53.1 us -> 9.39 us
  starting transfers between devices: 38.6 us -> 18 us
    scatter x7 -> x0, local copies, waits for them, and re-layouts: 174 us -> none  [the longest x1 72.1 us: reslot(): values.at[..., mode_count].set(jnp.where(first_pencil, new_imag, imag_part))]
    pallas_call x0 -> x1, Pallas kernels: none -> 110 us  [spectral(): pl.pallas_call(functools.partial(spectral_kernel, slabs), out_shape=jax.S...]
    dot_general x11 -> x5, matrix products: 91.5 us -> 25.7 us  [deposit(): lax.dot_general(spread, weight_y, (((0,), (0,)), ((), ())), precision=lax...]
    all_to_all x3 -> x0, waiting for transfers between devices: 53.7 us -> none  [the longest x1 26 us: on_device(): lax.all_to_all(spectral, 'gz', split_axis=2, concat_axis=1, tiled=True)]
    all_to_all x1 -> x0, blocking collectives: 46.1 us -> none  [on_device(): lax.all_to_all(physical, 'gz', split_axis=1, concat_axis=2, tiled=True)]
    unnamed x48 -> x7, local copies, waits for them, and re-layouts: 35.5 us -> 1.16 us
    all_to_all x4 -> x0, other arithmetic: 24.4 us -> none  [the longest x1 6.33 us: on_device(): lax.all_to_all(physical, 'gx', split_axis=2, concat_axis=3, tiled=True)]
    all_to_all x3 -> x0, starting transfers between devices: 20.9 us -> none  [the longest x1 11 us: on_device(): lax.all_to_all(spectral, 'gz', split_axis=2, concat_axis=1, tiled=True)]
  transfers between devices with their start and end apart: 13 -> 10, of which waited for: 12 -> 9; matrix products, arithmetic and copies ran while one was open for 3% -> 0% of each run, Pallas kernels for 0% -> 0%
where the time goes in v1:
time: 199 us; the launch traced here: 197 us
  Pallas kernels  110 us (55%)
  matrix products  25.7 us (13%)
  waiting for transfers between devices  20.9 us (11%)
  starting transfers between devices  18 us (9%)
  other arithmetic  9.39 us (5%)
  local copies, waits for them, and re-layouts  8.7 us (4%)
  between operations  4.06 us (2%)
    pallas_call x1, Pallas kernels, spectral(): pl.pallas_call(functools.partial(spectral_kernel, slabs), out_shape=jax.S...  110 us
    dot_general x5, matrix products, deposit(): lax.dot_general(spread, weight_y, (((0,), (0,)), ((), ())), precision=lax...  25.7 us
    ppermute x5, waiting for transfers between devices, padded_2(): lax.ppermute(tail, axis, [(i, (i + 1) % count) for i in range(count)])  14.4 us
    ppermute x5, starting transfers between devices, padded_2(): lax.ppermute(head, axis, [((i + 1) % count, i) for i in range(count)])  14.2 us
    ppermute x5, waiting for transfers between devices, padded_2(): lax.ppermute(head, axis, [((i + 1) % count, i) for i in range(count)])  6.52 us
  transfers between devices with their start and end apart: 10, of which 9 were waited for; matrix products, arithmetic and copies ran while one was open for 0% of the time, Pallas kernels for 0%

profile of v1, /device:TPU:8, one launch (start us, length us, event | category | flops | bytes accessed | tf_op | source)
XLA Modules:
  0.0 197.2 jit_solution(7219913254871920158)
XLA Ops:
  0.6 1.3 fusion.91
  4.6 0.7 convert_element_type.44
  5.2 1.3 compare_not_fusion
  7.2 0.8 and_select_fusion.4
  8.1 7.6 %collective-permute-start.1 = (f32[7,64]{1,0:T(8,128)S(1)}, f32[7,64]{1,0:T(8,128)S(1)}, u32[]{:S(2)}, u32[]{:S(2)}) collective-permute-start(f32[7,64]{1,0:T(8,128)S(1)} %get-tuple-element.216), channel_id=1, source_target_pairs={{4,0},{8,4},{12,8},{16,12},{20,16},{24,20},{28,24},{32,28},{36,32}... | collective-permute-start | bytes 5384 | tf_op jit(solution)/shard_map/ppermute | solution.py:336
  15.7 1.2 collective-permute-done
  17.1 28.1 %while.18 = (s32[]{:T(128)}, f32[2448,256]{1,0:T(8,128)}, f32[5,128,7]{1,2,0:T(8,128)S(1)}, s32[]{:T(128)}, s32[]{:T(128)}) while((s32[]{:T(128)}, f32[2448,256]{1,0:T(8,128)}, f32[5,128,7]{1,2,0:T(8,128)S(1)}, s32[]{:T(128)}, s32[]{:T(128)}) %tuple.75), condition=%wide.region_1.2_spmd.clone, body=%wide.region_0.1_spmd.clone.sunk | while | flops 965456192 | bytes 10168011 | solution.py:404
  17.5 3.8 %convolution_add_fusion.2 = f32[2448,256]{1,0:T(8,128)} fusion(f32[128,2448]{0,1:T(8,128)S(1)} %mul.605, f32[2448,256]{1,0:T(8,128)} %get-tuple-element.260, pred[]{:T(512)S(6)} %compare.46, f32[128]{0:T(128)S(1)} %get-tuple-element.252, s32[128]{0:T(128)S(1)} %get-tuple-element.253), kind=kOutput, calls=%fused_computation.3.clone.1 | convolution fusion | flops 964927488 | bytes 6267905 | tf_op jit(solution)/shard_map/while/body/eval_jaxpr/dot_general | solution.py:394
  21.8 5.5 %convolution_add_fusion.2 = f32[2448,256]{1,0:T(8,128)} fusion(f32[128,2448]{0,1:T(8,128)S(1)} %mul.605, f32[2448,256]{1,0:T(8,128)} %get-tuple-element.260, pred[]{:T(512)S(6)} %compare.46, f32[128]{0:T(128)S(1)} %get-tuple-element.252, s32[128]{0:T(128)S(1)} %get-tuple-element.253), kind=kOutput, calls=%fused_computation.3.clone.1 | convolution fusion | flops 964927488 | bytes 6267905 | tf_op jit(solution)/shard_map/while/body/eval_jaxpr/dot_general | solution.py:394
  27.8 5.5 %convolution_add_fusion.2 = f32[2448,256]{1,0:T(8,128)} fusion(f32[128,2448]{0,1:T(8,128)S(1)} %mul.605, f32[2448,256]{1,0:T(8,128)} %get-tuple-element.260, pred[]{:T(512)S(6)} %compare.46, f32[128]{0:T(128)S(1)} %get-tuple-element.252, s32[128]{0:T(128)S(1)} %get-tuple-element.253), kind=kOutput, calls=%fused_computation.3.clone.1 | convolution fusion | flops 964927488 | bytes 6267905 | tf_op jit(solution)/shard_map/while/body/eval_jaxpr/dot_general | solution.py:394
  33.7 5.5 %convolution_add_fusion.2 = f32[2448,256]{1,0:T(8,128)} fusion(f32[128,2448]{0,1:T(8,128)S(1)} %mul.605, f32[2448,256]{1,0:T(8,128)} %get-tuple-element.260, pred[]{:T(512)S(6)} %compare.46, f32[128]{0:T(128)S(1)} %get-tuple-element.252, s32[128]{0:T(128)S(1)} %get-tuple-element.253), kind=kOutput, calls=%fused_computation.3.clone.1 | convolution fusion | flops 964927488 | bytes 6267905 | tf_op jit(solution)/shard_map/while/body/eval_jaxpr/dot_general | solution.py:394
  39.7 5.5 %convolution_add_fusion.2 = f32[2448,256]{1,0:T(8,128)} fusion(f32[128,2448]{0,1:T(8,128)S(1)} %mul.605, f32[2448,256]{1,0:T(8,128)} %get-tuple-element.260, pred[]{:T(512)S(6)} %compare.46, f32[128]{0:T(128)S(1)} %get-tuple-element.252, s32[128]{0:T(128)S(1)} %get-tuple-element.253), kind=kOutput, calls=%fused_computation.3.clone.1 | convolution fusion | flops 964927488 | bytes 6267905 | tf_op jit(solution)/shard_map/while/body/eval_jaxpr/dot_general | solution.py:394
  45.2 2.4 %reshape.325 = f32[3,12,68,256]{3,2,1,0:T(8,128)S(1)} reshape(f32[2448,256]{1,0:T(8,128)} %get-tuple-element.166) | data formatting | bytes 5013504 | tf_op jit(solution)/shard_map/reshape | solution.py:405
  47.8 5.1 %collective-permute-start.3 = (f32[3,2,68,256]{3,2,1,0:T(8,128)S(1)}, f32[3,2,68,256]{3,2,1,0:T(8,128)S(1)}, u32[]{:S(2)}, u32[]{:S(2)}) collective-permute-start(f32[3,2,68,256]{3,2,1,0:T(8,128)S(1)} %get-tuple-element.200), channel_id=1, source_target_pairs={{4,0},{8,4},{12,8},{16,12},{20,16},{24,20},{28,24},{32,28},{36,32}... | collective-permute-start | bytes 1253384 | tf_op jit(solution)/shard_map/ppermute | solution.py:336
  53.0 5.8 %collective-permute-done.2 = f32[3,2,68,256]{3,2,1,0:T(8,128)S(1)} collective-permute-done((f32[3,2,68,256]{3,2,1,0:T(8,128)S(1)}, f32[3,2,68,256]{3,2,1,0:T(8,128)S(1)}, u32[]{:S(2)}, u32[]{:S(2)}) %collective-permute-start.2) | collective-permute-done | bytes 417824 | tf_op jit(solution)/shard_map/ppermute | solution.py:334
  59.0 1.7 collective-permute-start.4
  60.7 0.2 slice.276
  60.9 0.5 collective-permute-start.5
  61.4 1.8 collective-permute-done.4
  63.3 1.8 collective-permute-done.5
  65.2 1.3 add.151.vort
  66.5 110.1 %shard_map.149 = f32[3,8,64,256]{3,2,1,0:T(8,128)} custom-call(f32[3,8,64,256]{3,2,1,0:T(8,128)} %add.151.vort, bf16[4,2,256,256]{3,2,1,0:T(8,128)(2,1)} %constant.307.clone.ahead_y, bf16[4,2,256,256]{3,2,1,0:T(8,128)(2,1)} %constant.308.clone.back_y, bf16[2,512,512]{2,1,0:T(8,128)(2,1)} %constant.309.clone.ahead_x, ...), custom_call_target="tpu_custom_call" | custom-call | tf_op jit(solution)/shard_map/pallas_call | solution.py:302
  176.7 2.6 %fusion.89 = (f32[3,8,64,255]{3,2,1,0:T(8,128)S(1)}, f32[3,8,64,255]{3,2,1,0:T(8,128)S(1)}) fusion(f32[3,8,64,256]{3,2,1,0:T(8,128)} %shard_map.149), kind=kLoop, calls=%fused_computation.148 | loop fusion | bytes 6266880 | tf_op jit(solution)/shard_map/jit(_roll_static)/slice | solution.py:426
  179.3 0.9 collective-permute-start.6
  180.2 0.3 fusion.88
  180.5 2.9 %collective-permute-done.6 = f32[3,1,64,256]{3,2,1,0:T(8,128)S(1)} collective-permute-done((f32[3,1,64,256]{3,2,1,0:T(8,128)S(1)}, f32[3,1,64,256]{3,2,1,0:T(8,128)S(1)}, u32[]{:S(2)}, u32[]{:S(2)}) %collective-permute-start.6) | collective-permute-done | bytes 196640 | tf_op jit(solution)/shard_map/ppermute | solution.py:336
  183.4 5.2 %collective-permute-done.7 = f32[3,1,64,256]{3,2,1,0:T(8,128)S(1)} collective-permute-done((f32[3,1,64,256]{3,2,1,0:T(8,128)S(1)}, f32[3,1,64,256]{3,2,1,0:T(8,128)S(1)}, u32[]{:S(2)}, u32[]{:S(2)}) %collective-permute-start.7) | collective-permute-done | bytes 196640 | tf_op jit(solution)/shard_map/ppermute | solution.py:334
  188.8 2.0 %collective-permute-start.9 = (f32[3,10,1,256]{3,2,1,0:T(1,128)S(1)}, f32[3,10,1,256]{3,2,1,0:T(1,128)S(1)}, u32[]{:S(2)}, u32[]{:S(2)}) collective-permute-start(f32[3,10,1,256]{3,2,1,0:T(1,128)S(1)} %get-tuple-element.203), channel_id=1, source_target_pairs={{0,1},{1,2},{2,3},{3,0},{4,5},{5,6},{6,7},{7,4},{8,9},{9,10},{10,1... | collective-permute-start | bytes 92168 | tf_op jit(solution)/shard_map/ppermute | solution.py:334
  190.9 1.7 collective-permute-done.8
  192.6 0.4 collective-permute-done.9
  193.0 3.1 %fusion.74 = f32[3,8,64,256]{3,2,1,0:T(8,128)} fusion(f32[3,8,64,256]{3,2,1,0:T(8,128)S(1)} %copy-done.1, f32[3,10,1,256]{3,2,1,0:T(1,128)S(1)} %collective-permute-done.9, f32[3,1,64,256]{3,2,1,0:T(8,128)S(1)} %collective-permute-done.6, f32[3,8,64,256]{3,2,1,0:T(8,128)S(1)} %copy-done, f32[3,1,64,256]{3,2,1,0:T(8,128)S(1)} %collective-permute-done.7, ...), kind=kLoop, calls=%fused_computation.106 | loop fusion | flops 7864320 | bytes 9891840 | tf_op jit(solution)/shard_map/add | solution.py:430
  196.1 1.1 copy.28
  (88 shorter events, 3.3 us)
Async XLA Ops:
  8.1 8.8 %collective-permute-start = (f32[7,64]{1,0:T(8,128)S(1)}, f32[7,64]{1,0:T(8,128)S(1)}, u32[]{:S(2)}, u32[]{:S(2)}) collective-permute-start(f32[7,64]{1,0:T(8,128)S(1)} %get-tuple-element.215), channel_id=1, source_target_pairs={{0,4},{4,8},{8,12},{12,16},{16,20},{20,24},{24,28},{28,32},{32,36}... | collective-permute-start | bytes 5384 | tf_op jit(solution)/shard_map/ppermute | solution.py:334
  8.1 8.9 %collective-permute-start.1 = (f32[7,64]{1,0:T(8,128)S(1)}, f32[7,64]{1,0:T(8,128)S(1)}, u32[]{:S(2)}, u32[]{:S(2)}) collective-permute-start(f32[7,64]{1,0:T(8,128)S(1)} %get-tuple-element.216), channel_id=1, source_target_pairs={{4,0},{8,4},{12,8},{16,12},{20,16},{24,20},{28,24},{32,28},{36,32}... | collective-permute-start | bytes 5384 | tf_op jit(solution)/shard_map/ppermute | solution.py:336
  47.7 11.1 %collective-permute-start.2 = (f32[3,2,68,256]{3,2,1,0:T(8,128)S(1)}, f32[3,2,68,256]{3,2,1,0:T(8,128)S(1)}, u32[]{:S(2)}, u32[]{:S(2)}) collective-permute-start(f32[3,2,68,256]{3,2,1,0:T(8,128)S(1)} %get-tuple-element.201), channel_id=1, source_target_pairs={{0,4},{4,8},{8,12},{12,16},{16,20},{20,24},{24,28},{28,32},{32,36}... | collective-permute-start | bytes 1253384 | tf_op jit(solution)/shard_map/ppermute | solution.py:334
  47.8 11.1 %collective-permute-start.3 = (f32[3,2,68,256]{3,2,1,0:T(8,128)S(1)}, f32[3,2,68,256]{3,2,1,0:T(8,128)S(1)}, u32[]{:S(2)}, u32[]{:S(2)}) collective-permute-start(f32[3,2,68,256]{3,2,1,0:T(8,128)S(1)} %get-tuple-element.200), channel_id=1, source_target_pairs={{4,0},{8,4},{12,8},{16,12},{20,16},{24,20},{28,24},{32,28},{36,32}... | collective-permute-start | bytes 1253384 | tf_op jit(solution)/shard_map/ppermute | solution.py:336
  59.0 6.1 %copy-start.2 = (f32[3,8,64,256]{3,2,1,0:T(8,128)S(1)}, f32[3,8,64,256]{3,2,1,0:T(8,128)}, u32[]{:S(2)}) copy-start(f32[3,8,64,256]{3,2,1,0:T(8,128)} %param.28) | copy-start | bytes 4718596
  59.0 4.2 %collective-permute-start.4 = (f32[3,8,2,256]{3,2,1,0:T(2,128)S(1)}, f32[3,8,2,256]{3,2,1,0:T(2,128)S(1)}, u32[]{:S(2)}, u32[]{:S(2)}) collective-permute-start(f32[3,8,2,256]{3,2,1,0:T(2,128)S(1)} %get-tuple-element.205), channel_id=1, source_target_pairs={{0,1},{1,2},{2,3},{3,0},{4,5},{5,6},{6,7},{7,4},{8,9},{9,10},{10,1... | collective-permute-start | bytes 147464 | tf_op jit(solution)/shard_map/ppermute | solution.py:334
  60.9 4.2 %collective-permute-start.5 = (f32[3,8,2,256]{3,2,1,0:T(2,128)S(1)}, f32[3,8,2,256]{3,2,1,0:T(2,128)S(1)}, u32[]{:S(2)}, u32[]{:S(2)}) collective-permute-start(f32[3,8,2,256]{3,2,1,0:T(2,128)S(1)} %get-tuple-element.204), channel_id=1, source_target_pairs={{1,0},{2,1},{3,2},{0,3},{5,4},{6,5},{7,6},{4,7},{9,8},{10,9},{11,1... | collective-permute-start | bytes 147464 | tf_op jit(solution)/shard_map/ppermute | solution.py:336
  176.7 2.6 %copy-start = (f32[3,8,64,256]{3,2,1,0:T(8,128)S(1)}, f32[3,8,64,256]{3,2,1,0:T(8,128)}, u32[]{:S(2)}) copy-start(f32[3,8,64,256]{3,2,1,0:T(8,128)} %shard_map.149) | copy-start | bytes 4718596
  179.3 4.1 %collective-permute-start.6 = (f32[3,1,64,256]{3,2,1,0:T(8,128)S(1)}, f32[3,1,64,256]{3,2,1,0:T(8,128)S(1)}, u32[]{:S(2)}, u32[]{:S(2)}) collective-permute-start(f32[3,1,64,256]{3,2,1,0:T(8,128)S(1)} %get-tuple-element.214), channel_id=1, source_target_pairs={{4,0},{8,4},{12,8},{16,12},{20,16},{24,20},{28,24},{32,28},{36,32}... | collective-permute-start | bytes 589832 | tf_op jit(solution)/shard_map/ppermute | solution.py:336
  180.2 8.4 %collective-permute-start.7 = (f32[3,1,64,256]{3,2,1,0:T(8,128)S(1)}, f32[3,1,64,256]{3,2,1,0:T(8,128)S(1)}, u32[]{:S(2)}, u32[]{:S(2)}) collective-permute-start(f32[3,1,64,256]{3,2,1,0:T(8,128)S(1)} %get-tuple-element.213), channel_id=1, source_target_pairs={{0,4},{4,8},{8,12},{12,16},{16,20},{20,24},{24,28},{28,32},{32,36}... | collective-permute-start | bytes 589832 | tf_op jit(solution)/shard_map/ppermute | solution.py:334
  180.5 10.3 %copy-start.1 = (f32[3,8,64,256]{3,2,1,0:T(8,128)S(1)}, f32[3,8,64,256]{3,2,1,0:T(8,128)}, u32[]{:S(2)}) copy-start(f32[3,8,64,256]{3,2,1,0:T(8,128)} %add.151.vort) | copy-start | bytes 4718596
  188.7 4.0 %collective-permute-start.8 = (f32[3,10,1,256]{3,2,1,0:T(1,128)S(1)}, f32[3,10,1,256]{3,2,1,0:T(1,128)S(1)}, u32[]{:S(2)}, u32[]{:S(2)}) collective-permute-start(f32[3,10,1,256]{3,2,1,0:T(1,128)S(1)} %get-tuple-element.202), channel_id=1, source_target_pairs={{1,0},{2,1},{3,2},{0,3},{5,4},{6,5},{7,6},{4,7},{9,8},{10,9},{11,1... | collective-permute-start | bytes 92168 | tf_op jit(solution)/shard_map/ppermute | solution.py:336
  188.8 4.3 %collective-permute-start.9 = (f32[3,10,1,256]{3,2,1,0:T(1,128)S(1)}, f32[3,10,1,256]{3,2,1,0:T(1,128)S(1)}, u32[]{:S(2)}, u32[]{:S(2)}) collective-permute-start(f32[3,10,1,256]{3,2,1,0:T(1,128)S(1)} %get-tuple-element.203), channel_id=1, source_target_pairs={{0,1},{1,2},{2,3},{3,0},{4,5},{5,6},{6,7},{7,4},{8,9},{9,10},{10,1... | collective-permute-start | bytes 92168 | tf_op jit(solution)/shard_map/ppermute | solution.py:334

commit v2 on v1

--- a/solution.py
+++ b/solution.py
@@ -17,6 +17,11 @@
 MODES = 32
 PLANES = 8
 KXS = 4
+NY = 256
+PART = 512
+OWN = 640
+LANES = 1792
+HOPS = ((1, 0, 128, 512), (1, 128, 384, 128), (-1, 0, 128, 1152), (-1, 128, 384, 1280), (2, 0, 128, 0), (-2, 0, 128, 1664))
 
 
 def halves(table):
@@ -74,6 +79,13 @@
     )
 
 
+def kernel_weight(distance):
+    radius = jnp.abs(distance)
+    near_part = 1.0 - 2.5 * radius * radius + 1.5 * radius * radius * radius
+    far_part = 0.5 * (2.0 - radius) * (2.0 - radius) * (1.0 - radius)
+    return jnp.where(radius < 1.0, near_part, jnp.where(radius < 2.0, far_part, 0.0))
+
+
 def split(values):
     high = values.astype(BF16)
     return high, (values - high.astype(F32)).astype(BF16)
@@ -93,9 +105,14 @@
     return dot(high, table[0]) + (dot(low, table[0]) + dot(high, table[1]))
 
 
-def spectral_kernel(
-    slabs, vort, ahead_y, back_y, ahead_x, back_x, ahead_1, back_1, ahead_2, back_2, twiddle,
-    vel, ys, xr, xo, zr, spec, zo, xr2, xo2, yr, send_sem, recv_sem, own_sem,
+def step_kernel(
+    slabs, counts, strength, offsets, cells, ambient,
+    ahead_y, back_y, ahead_x, back_x, ahead_1, back_1, ahead_2, back_2, twiddle,
+    vel, vorticity,
+    packet, wide_x, high_y, low_y, high_l, low_l, rim, rim_in, vort, plane_in, side, side_in,
+    ys, xr, xo, zr, spec, zo, xr2, xo2, yr,
+    send_sem, recv_sem, own_sem, packet_send, packet_recv, rim_send, rim_recv,
+    plane_send, plane_recv, side_send, side_recv,
 ):
     me_z, me_x = lax.axis_index("gz"), lax.axis_index("gx")
     nx = 4 * slabs
@@ -114,7 +131,100 @@
     lax.fori_loop(1, slabs, greet, 0)
     for i in range(1, PENCILS):
         pl.semaphore_signal(barrier, inc=1, device_id={"gx": lax.rem(me_x + i, PENCILS)}, device_id_type=MESH)
+    lane_id = lax.broadcasted_iota(jnp.int32, (1, PART), 1)
+    up, down = counts[0], counts[1]
+    moves = jnp.where(lane_id < up, 1, jnp.where(lane_id < up + down, -1, 0))
+    cell = cells[...]
+    packet[:, OWN:OWN + PART] = jnp.concatenate(
+        [
+            strength[...],
+            offsets[...],
+            (cell // (xl * NY) + PLANES * moves).astype(F32),
+            (cell % (xl * NY)).astype(F32),
+        ],
+        axis=0,
+    )
     pl.semaphore_wait(barrier, slabs - 1 + PENCILS - 1)
+
+    hops = []
+    for n, (far, start, width, land) in enumerate(HOPS):
+        hop = pltpu.make_async_remote_copy(
+            src_ref=packet.at[:, OWN + start:OWN + start + width],
+            dst_ref=packet.at[:, land:land + width],
+            send_sem=packet_send.at[n],
+            recv_sem=packet_recv.at[n],
+            device_id={"gz": lax.rem(me_z + far + slabs, slabs)},
+            device_id_type=MESH,
+        )
+        hop.start()
+        hops.append(hop)
+    for hop in hops:
+        hop.wait_recv()
+    fields = packet[...]
+    lane = lax.broadcasted_iota(jnp.int32, (1, LANES), 1)
+    shift = jnp.where(lane < 128, -16.0, jnp.where(lane < OWN, -8.0, jnp.where(lane < OWN + PART, 0.0, jnp.where(lane < LANES - 128, 8.0, 16.0))))
+    z_cell = fields[6:7] + shift
+    lateral = fields[7:8].astype(jnp.int32)
+    x_cell = (lateral // NY).astype(F32)
+    y_cell = lateral % NY
+    plane = lax.broadcasted_iota(jnp.int32, (PLANES, LANES), 0).astype(F32)
+    weight_z = kernel_weight((plane - z_cell) - fields[3:4])
+    row = lax.broadcasted_iota(jnp.int32, (xl, LANES), 0).astype(F32)
+    wide_x[...] = kernel_weight((row - x_cell) - fields[4:5])
+    at_y = lax.broadcasted_iota(jnp.int32, (NY, LANES), 0)
+    away = (at_y - y_cell + NY // 2) % NY - NY // 2
+    weight_y = kernel_weight(away.astype(F32) - fields[5:6])
+    high, low = split(weight_y)
+    high_y[...] = high
+    low_y[...] = low
+    charge = [fields[c:c + 1] * weight_z for c in range(3)]
+
+    def spread_over_y(high, low, lo, hi):
+        def times(a, b):
+            return lax.dot_general(a, b, (((1,), (1,)), ((), ())), preferred_element_type=F32)
+
+        top = high_y[:, lo:hi]
+        return times(high, top) + (times(low, top) + times(high, low_y[:, lo:hi]))
+
+    rims = []
+    for n, first in enumerate((xl, -2)):
+        beyond = []
+        for c in range(3):
+            for r in range(2):
+                beyond.append(charge[c] * kernel_weight((float(first + r) - x_cell) - fields[4:5]))
+        high, low = split(jnp.concatenate(beyond, axis=0))
+        rim[n] = spread_over_y(high, low, 0, LANES)
+        far = 1 if n == 0 else PENCILS - 1
+        copy = pltpu.make_async_remote_copy(
+            src_ref=rim.at[n],
+            dst_ref=rim_in.at[n],
+            send_sem=rim_send.at[n],
+            recv_sem=rim_recv.at[n],
+            device_id={"gx": lax.rem(me_x + far, PENCILS)},
+            device_id_type=MESH,
+        )
+        copy.start()
+        rims.append(copy)
+
+    def deposit(c):
+        for planes, lo, hi in ((range(0, 2), 0, 1280), (range(2, 6), 512, 1280), (range(6, 8), 512, 1792)):
+            columns = wide_x[:, lo:hi]
+            for n, z in enumerate(planes):
+                high, low = split(columns * charge[c][z:z + 1, lo:hi])
+                high_l[n * xl:(n + 1) * xl, 0:hi - lo] = high
+                low_l[n * xl:(n + 1) * xl, 0:hi - lo] = low
+            size = len(planes) * xl
+            added = spread_over_y(high_l[0:size, 0:hi - lo], low_l[0:size, 0:hi - lo], lo, hi)
+            for n, z in enumerate(planes):
+                vort[c, z] = ambient[c, z] + added[n * xl:(n + 1) * xl]
+        if c == 0:
+            for copy in rims:
+                copy.wait_recv()
+        for n, first in enumerate((0, xl - 2)):
+            for r in range(2):
+                for z in range(PLANES):
+                    at = c * 16 + r * 8 + z
+                    vort[c, z, first + r:first + r + 1, :] += rim_in[n, at:at + 1, :]
 
     def own_copy(src, dst, c, stage, width, index):
         at = pl.ds(pl.multiple_of(index * width, 8), width)
@@ -168,10 +278,11 @@
         pltpu.make_async_copy(window, window, send_sem.at[stage, c]).wait()
 
     for c in range(3):
+        deposit(c)
         spread = []
         for r in range(4):
-            cells = jnp.concatenate([vort[c, r], vort[c, r + 4]], axis=0)
-            spread.append(times_table(cells, ahead_y[r]))
+            both = jnp.concatenate([vort[c, r], vort[c, r + 4]], axis=0)
+            spread.append(times_table(both, ahead_y[r]))
         spot = lax.broadcasted_iota(jnp.int32, (part, 128), 1) // MODES
         for b in range(PENCILS):
             for p in range(2):
@@ -265,6 +376,7 @@
         xo2[c] = table_times(back_x, xr2[c])
         send_gx(xo2, yr, c, 3)
     spot = lax.broadcasted_iota(jnp.int32, (xl, 128), 1) // MODES
+    edges = [[], [], []]
     for c in range(3):
         arrive(xo2, yr, c, 3)
         rolled = {}
@@ -284,9 +396,51 @@
                         picked = jnp.where(spot == (b + r) % 4, rolled[zh, b, p], picked)
                     both.append(picked)
                 sides.append(jnp.concatenate(both, axis=1))
-            cells = times_table(jnp.concatenate(sides, axis=0), back_y[r])
-            vel[c, r] = cells[:xl]
-            vel[c, r + 4] = cells[xl:]
+            both = times_table(jnp.concatenate(sides, axis=0), back_y[r])
+            vel[c, r] = both[:xl]
+            vel[c, r + 4] = both[xl:]
+        for n, (far, z) in enumerate(((1, PLANES - 1), (slabs - 1, 0))):
+            copy = pltpu.make_async_remote_copy(
+                src_ref=vel.at[c, z],
+                dst_ref=plane_in.at[n, c],
+                send_sem=plane_send.at[n, c],
+                recv_sem=plane_recv.at[n, c],
+                device_id={"gz": lax.rem(me_z + far, slabs)},
+                device_id_type=MESH,
+            )
+            copy.start()
+            edges[c].append(copy)
+        for n, (far, x) in enumerate(((1, xl - 1), (PENCILS - 1, 0))):
+            side[n, c] = jnp.concatenate([vel[c, z, x:x + 1, :] for z in range(PLANES)], axis=0)
+            copy = pltpu.make_async_remote_copy(
+                src_ref=side.at[n, c],
+                dst_ref=side_in.at[n, c],
+                send_sem=side_send.at[n, c],
+                recv_sem=side_recv.at[n, c],
+                device_id={"gx": lax.rem(me_x + far, PENCILS)},
+                device_id_type=MESH,
+            )
+            copy.start()
+            edges[c].append(copy)
+    at_x = lax.broadcasted_iota(jnp.int32, (xl, NY), 0)
+    for c in range(3):
+        for copy in edges[c]:
+            copy.wait_recv()
+        for z in range(PLANES):
+            here = vel[c, z]
+            above = vel[c, z + 1] if z < PLANES - 1 else plane_in[1, c]
+            below = vel[c, z - 1] if z > 0 else plane_in[0, c]
+            right = jnp.where(at_x == xl - 1, side_in[1, c, z:z + 1, :], pltpu.roll(here, xl - 1, 0))
+            left = jnp.where(at_x == 0, side_in[0, c, z:z + 1, :], pltpu.roll(here, 1, 0))
+            turned = pltpu.roll(here, NY - 1, 1) - pltpu.roll(here, 1, 1)
+            stretch = (
+                vort[0, z] * ((above - below) * 0.5)
+                + vort[1, z] * ((right - left) * 0.5)
+                + vort[2, z] * (turned * 0.5)
+            )
+            vorticity[c, z] = vort[c, z] + 0.25 * stretch
+    for copy in hops + rims + edges[0] + edges[1] + edges[2]:
+        copy.wait_send()
     for c in range(3):
         sent(ys, c, 0)
         sent(xo, c, 1)
@@ -294,140 +448,45 @@
         sent(xo2, c, 3)
 
 
-def spectral(vort, slabs):
+def on_device(strength, offsets, cell_index, migrate_count, ambient):
+    slabs = lax.axis_size("gz")
+    xl = ambient.shape[2]
     consts = [jnp.asarray(t) for t in tables(slabs)]
     rows = 8 * slabs
     lanes = PLANES * MODES
     wide = pltpu.VMEM((3, rows, lanes), F32)
+    dma = pltpu.SemaphoreType.DMA
+    vmem = pl.BlockSpec(memory_space=pltpu.VMEM)
+    mesh = jax.ShapeDtypeStruct(ambient.shape, F32)
     return pl.pallas_call(
-        functools.partial(spectral_kernel, slabs),
-        out_shape=jax.ShapeDtypeStruct(vort.shape, F32),
-        in_specs=[pl.BlockSpec(memory_space=pltpu.VMEM)] * (1 + len(consts)),
-        out_specs=pl.BlockSpec(memory_space=pltpu.VMEM),
+        functools.partial(step_kernel, slabs),
+        out_shape=(mesh, mesh),
+        in_specs=[pl.BlockSpec(memory_space=pltpu.SMEM)] + [vmem] * (4 + len(consts)),
+        out_specs=(vmem, vmem),
         scratch_shapes=[
+            pltpu.VMEM((8, LANES), F32),
+            pltpu.VMEM((xl, LANES), F32),
+            pltpu.VMEM((NY, LANES), BF16),
+            pltpu.VMEM((NY, LANES), BF16),
+            pltpu.VMEM((4 * xl, 1280), BF16),
+            pltpu.VMEM((4 * xl, 1280), BF16),
+            pltpu.VMEM((2, 48, NY), F32),
+            pltpu.VMEM((2, 48, NY), F32),
+            pltpu.VMEM((3, PLANES, xl, NY), F32),
+            pltpu.VMEM((2, 3, xl, NY), F32),
+            pltpu.VMEM((2, 3, PLANES, NY), F32),
+            pltpu.VMEM((2, 3, PLANES, NY), F32),
             wide, wide, wide, wide,
             pltpu.VMEM((3, 4 * slabs, 2 * lanes), F32),
             wide, wide, wide, wide,
-            pltpu.SemaphoreType.DMA((4, 3)),
-            pltpu.SemaphoreType.DMA((4, 3)),
-            pltpu.SemaphoreType.DMA((4, 3)),
+            dma((4, 3)), dma((4, 3)), dma((4, 3)),
+            dma((6,)), dma((6,)), dma((2,)), dma((2,)),
+            dma((2, 3)), dma((2, 3)), dma((2, 3)), dma((2, 3)),
         ],
         compiler_params=pltpu.CompilerParams(
-            collective_id=0, has_side_effects=True, vmem_limit_bytes=56 * 1024 * 1024
+            collective_id=0, has_side_effects=True, vmem_limit_bytes=60 * 1024 * 1024
         ),
-    )(vort, *consts)
-
-
-NY = 256
-PART = 512
-MIG = 64
-time_step = 0.25
-
-
-def padded_2(cells, sides, width):
-    for axis, dim in sides:
-        count = lax.axis_size(axis)
-        head = lax.slice_in_dim(cells, 0, width, axis=dim)
-        tail = lax.slice_in_dim(cells, cells.shape[dim] - width, cells.shape[dim], axis=dim)
-        cells = jnp.concatenate(
-            [
-                lax.ppermute(tail, axis, [(i, (i + 1) % count) for i in range(count)]),
-                cells,
-                lax.ppermute(head, axis, [((i + 1) % count, i) for i in range(count)]),
-            ],
-            axis=dim,
-        )
-    return cells
-
-
-def kernel_weight(distance):
-    radius = jnp.abs(distance)
-    near_part = 1.0 - 2.5 * radius * radius + 1.5 * radius * radius * radius
-    far_part = 0.5 * (2.0 - radius) * (2.0 - radius) * (1.0 - radius)
-    return jnp.where(radius < 1.0, near_part, jnp.where(radius < 2.0, far_part, 0.0))
-
-
-def on_device(strength, offsets, cell_index, migrate_count, ambient):
-    slab_planes = ambient.shape[1]
-    pencil_cols = ambient.shape[2]
-    slab_count = lax.axis_size("gz")
-    up_count = migrate_count[0, 0, 0]
-    down_count = migrate_count[0, 0, 1]
-    slot_index = jnp.arange(PART, dtype=jnp.int32)
-    packet = jnp.concatenate([strength, offsets, cell_index.astype(jnp.float32)[None, :]], axis=0)
-    is_strength = (jnp.arange(7) < 3)[:, None]
-    head_live = slot_index[:MIG] < up_count
-    upward = jnp.where(is_strength & ~head_live[None, :], 0.0, packet[:, :MIG])
-    downward = lax.dynamic_slice_in_dim(packet, up_count, MIG, axis=1)
-    down_live = jnp.arange(MIG, dtype=jnp.int32) < down_count
-    downward = jnp.where(is_strength & ~down_live[None, :], 0.0, downward)
-    outgoing = jnp.concatenate([downward, upward], axis=1)
-    extended = padded_2(outgoing, (("gz", 1),), MIG)
-    arrived = jnp.concatenate([extended[:, :MIG], extended[:, 3 * MIG :]], axis=1)
-    staying = slot_index >= up_count + down_count
-    retained = jnp.where(is_strength & ~staying[None, :], 0.0, packet)
-    particles = jnp.concatenate([retained, arrived], axis=1)
-    particle_total = particles.shape[1]
-    block_rows = math.gcd(particle_total, 256)
-    row_blocks = particles.T.reshape(particle_total // block_rows, block_rows, 7)
-    planes = jnp.arange(slab_planes + 4, dtype=jnp.int32) - 2
-    columns = jnp.arange(pencil_cols + 4, dtype=jnp.int32) - 2
-    lateral = jnp.arange(NY, dtype=jnp.int32)
-
-    def deposit(deposited, row_group):
-        cell_ids = row_group[:, 6].astype(jnp.int32)
-        z_cell = cell_ids // (pencil_cols * NY)
-        x_cell = cell_ids // NY % pencil_cols
-        y_cell = cell_ids % NY
-        weight_z = kernel_weight(
-            (planes[None, :] - z_cell[:, None]).astype(jnp.float32) - row_group[:, 3:4]
-        )
-        weight_x = kernel_weight(
-            (columns[None, :] - x_cell[:, None]).astype(jnp.float32) - row_group[:, 4:5]
-        )
-        y_offset = (lateral[None, :] - y_cell[:, None] + NY // 2) % NY - NY // 2
-        weight_y = kernel_weight(y_offset.astype(jnp.float32) - row_group[:, 5:6])
-        spread = (
-            row_group[:, 0:3, None, None] * weight_z[:, None, :, None] * weight_x[:, None, None, :]
-        )
-        spread = spread.reshape(block_rows, -1)
-        added = lax.dot_general(
-            spread,
-            weight_y,
-            (((0,), (0,)), ((), ())),
-            precision=lax.Precision.HIGHEST,
-            preferred_element_type=jnp.float32,
-        )
-        return (deposited + added, None)
-
-    start_mesh = jnp.zeros((3 * (slab_planes + 4) * (pencil_cols + 4), NY), jnp.float32)
-    deposited, _ = lax.scan(deposit, start_mesh, row_blocks)
-    deposited = deposited.reshape(3, slab_planes + 4, pencil_cols + 4, NY)
-    plane_rim = jnp.concatenate([deposited[:, :2], deposited[:, slab_planes + 2 :]], axis=1)
-    plane_rim = padded_2(plane_rim, (("gz", 1),), 2)
-    interior = deposited[:, 2 : slab_planes + 2]
-    interior = (
-        interior.at[:, :2].add(plane_rim[:, :2]).at[:, slab_planes - 2 :].add(plane_rim[:, 6:])
-    )
-    column_rim = jnp.concatenate([interior[:, :, :2], interior[:, :, pencil_cols + 2 :]], axis=2)
-    column_rim = padded_2(column_rim, (("gx", 2),), 2)
-    interior = interior[:, :, 2 : pencil_cols + 2]
-    interior = (
-        interior.at[:, :, :2]
-        .add(column_rim[:, :, :2])
-        .at[:, :, pencil_cols - 2 :]
-        .add(column_rim[:, :, 6:])
-    )
-    vorticity_mesh = ambient + interior
-    velocity = spectral(vorticity_mesh, slab_count)
-    padded = padded_2(velocity, (("gz", 1), ("gx", 2)), 1)
-    along_z = (padded[:, 2:, 1:-1] - padded[:, :-2, 1:-1]) * 0.5
-    along_x = (padded[:, 1:-1, 2:] - padded[:, 1:-1, :-2]) * 0.5
-    along_y = (jnp.roll(velocity, -1, axis=3) - jnp.roll(velocity, 1, axis=3)) * 0.5
-    stretch = (
-        vorticity_mesh[0] * along_z + vorticity_mesh[1] * along_x + vorticity_mesh[2] * along_y
-    )
-    return (velocity, vorticity_mesh + time_step * stretch)
+    )(migrate_count.reshape(2), strength, offsets, cell_index.reshape(1, PART), ambient, *consts)
 
 
 def solution(mesh):

time: 199 us -> 137 us (0.69)
  matrix products: 25.7 us -> 0 us
  waiting for transfers between devices: 20.9 us -> 0 us
  Pallas kernels: 110 us -> 130 us
  starting transfers between devices: 18 us -> 0 us
  other arithmetic: 9.39 us -> 0 us
  local copies, waits for them, and re-layouts: 8.7 us -> 3.97 us
  between operations: 4.06 us -> 0.65 us
    dot_general x5 -> x0, matrix products: 25.7 us -> none  [deposit(): lax.dot_general(spread, weight_y, (((0,), (0,)), ((), ())), precision=lax...]
    ppermute x10 -> x0, waiting for transfers between devices: 20.9 us -> none  [the longest x5 14.4 us: padded_2(): lax.ppermute(tail, axis, [(i, (i + 1) % count) for i in range(count)])]
    pallas_call x1, Pallas kernels: 110 us -> 130 us  [on_device(): pl.pallas_call(functools.partial(step_kernel, slabs), out_shape=(mesh, me...]
    ppermute x10 -> x0, starting transfers between devices: 18 us -> none  [the longest x5 14.2 us: padded_2(): lax.ppermute(head, axis, [((i + 1) % count, i) for i in range(count)])]
    slice x13 -> x0, local copies, waits for them, and re-layouts: 4.64 us -> none  [the longest x2 2.87 us: on_device(): jnp.roll(velocity, 1, axis=3)]
    add x2 -> x0, other arithmetic: 4.42 us -> none  [the longest x1 3.07 us: on_device(): return (velocity, vorticity_mesh + time_step * stretch)]
    unnamed x7 -> x4, local copies, waits for them, and re-layouts: 1.16 us -> 3.97 us
    reshape x1 -> x0, local copies, waits for them, and re-layouts: 2.43 us -> none  [on_device(): deposited = deposited.reshape(3, slab_planes + 4, pencil_cols + 4, NY)]
  transfers between devices with their start and end apart: 10 -> 0, of which waited for: 9 -> 0; matrix products, arithmetic and copies ran while one was open for 0% -> 0% of each run, Pallas kernels for 0% -> 0%
where the time goes in v2:
time: 137 us; the launch traced here: 135 us
  Pallas kernels  130 us (95%)
  local copies, waits for them, and re-layouts  3.97 us (3%)
    pallas_call x1, Pallas kernels, on_device(): pl.pallas_call(functools.partial(step_kernel, slabs), out_shape=(mesh, me...  130 us
    unnamed x4, local copies, waits for them, and re-layouts  3.97 us

profile of v2, /device:TPU:8, one launch (start us, length us, event | category | flops | bytes accessed | tf_op | source)
XLA Modules:
  0.0 134.7 jit_solution(3105912981055722543)
XLA Ops:
  0.6 130.1 %shard_map.149 = (f32[3,8,64,256]{3,2,1,0:T(8,128)}, f32[3,8,64,256]{3,2,1,0:T(8,128)}) custom-call(s32[2]{0:T(128)} %bitcast.3, f32[3,512]{1,0:T(4,128)} %strength.1, f32[3,512]{1,0:T(4,128)} %offsets.1, s32[1,512]{1,0:T(1,128)} %bitcast.2, f32[3,8,64,256]{3,2,1,0:T(8,128)} %ambient.1, bf16[4,2,256,256]{3,2,1,0:T(8,128)(2,1)} %constant.18.clone.ahead_y, ...), custom_call_target="tpu_custom_call" | custom-call | tf_op jit(solution)/shard_map/pallas_call | solution.py:461
  130.7 0.0 copy-start
  130.8 2.8 %copy.18 = f32[3,8,64,256]{3,2,1,0:T(8,128)} copy(f32[3,8,64,256]{3,2,1,0:T(8,128)} %get-tuple-element.4) | data formatting | bytes 3145728
  133.6 0.0 copy-done
  133.6 1.1 copy.19
Async XLA Ops:
  130.7 2.8 %copy-start = (f32[3,8,64,256]{3,2,1,0:T(8,128)S(1)}, f32[3,8,64,256]{3,2,1,0:T(8,128)}, u32[]{:S(2)}) copy-start(f32[3,8,64,256]{3,2,1,0:T(8,128)} %get-tuple-element.5) | copy-start | bytes 4718596

commit v3 on v2

v3 whole, which is shorter than its diff:
```python
import functools
import math

import jax
import jax.numpy as jnp
import ml_dtypes
import numpy as np
from jax import lax
from jax.experimental import pallas as pl
from jax.experimental.pallas import tpu as pltpu
from jax.sharding import PartitionSpec as P

MESH = pl.DeviceIdType.MESH
F32 = jnp.float32
BF16 = jnp.bfloat16
PENCILS = 4
PLANES = 8
MODES = 16
KXS = 4
NY = 256
PART = 512
CHUNKS = 6
OWN = 640
LANES = 1792
HOPS = ((1, 0, 128, 512), (1, 128, 384, 128), (-1, 0, 128, 1152), (-1, 128, 384, 1280), (2, 0, 128, 0), (-2, 0, 128, 1664))


def halves(table):
    high = table.astype(ml_dtypes.bfloat16)
    low = (table - high.astype(np.float64)).astype(ml_dtypes.bfloat16)
    return np.stack([high, low])


def real_form(angle):
    cosine, sine = np.cos(angle), np.sin(angle)
    return np.stack([np.stack([cosine, sine], -1), np.stack([-sine, cosine], -1)], -2)


def kx_of(slabs):
    base = 2 * np.arange(slabs)
    rows = np.stack([base, base + 1, -base, -base - 1], 1) % (4 * slabs)
    rows[0, 2] = 2 * slabs
    return rows


def tables(slabs):
    nx, nz = 4 * slabs, 8 * slabs
    rows = 8 * slabs
    two_pi = 2.0 * np.pi
    y = np.arange(NY)
    half, pencil, mode = np.meshgrid(np.arange(2), np.arange(PENCILS), np.arange(MODES), indexing="ij")
    ky = (pencil * 2 * MODES + half * MODES + mode).reshape(-1)
    angle = two_pi * (y[:, None] * ky[None, :] % NY) / NY
    sine = np.where(ky[None, :] == 0, (1.0 - 2.0 * (y % 2))[:, None], -np.sin(angle))
    table_y = np.concatenate([np.cos(angle), sine], 1)
    weight = np.where(ky == 0, 1.0, 2.0) / NY
    back_y = table_y.T * np.concatenate([weight, weight])[:, None]
    kx = kx_of(slabs).reshape(-1)
    x = np.arange(nx)
    form = real_form(two_pi * (kx[:, None] * x[None, :] % nx) / nx)
    form = form.reshape(nx, PENCILS, nx // PENCILS, 2, 2).transpose(0, 3, 1, 4, 2)
    table_x = form.reshape(rows, rows)
    k1 = np.arange(slabs)
    form = real_form(two_pi * (k1[:, None] * k1[None, :] % slabs) / slabs)
    table_1 = np.einsum("ksoi,ab->okasbi", form, np.eye(KXS)).reshape(rows, rows)
    k2 = np.arange(PLANES)
    form = real_form(two_pi * (k2[:, None] * k2[None, :] % PLANES) / PLANES)
    table_2 = np.einsum("kpoi,ab->ipaokb", form, np.eye(MODES)).reshape(2 * PLANES * MODES, -1)
    angle = two_pi * (k1[:, None] * k2[None, :]) / nz
    angle = np.repeat(np.repeat(angle, KXS, 0), MODES, 1)
    twiddle = np.stack([np.cos(angle), np.sin(angle)]).astype(np.float32)
    return (
        halves(table_y), halves(back_y), halves(table_x), halves(table_x.T / nx),
        halves(table_1), halves(table_1.T / nz), halves(table_2), halves(table_2.T), twiddle,
    )


def kernel_weight(distance):
    radius = jnp.abs(distance)
    near_part = 1.0 + radius * radius * (1.5 * radius - 2.5)
    beyond = 2.0 - radius
    far_part = 0.5 * beyond * beyond * (1.0 - radius)
    return jnp.where(radius < 1.0, near_part, jnp.where(radius < 2.0, far_part, 0.0))


def split(values):
    high = values.astype(BF16)
    return high, (values - high.astype(F32)).astype(BF16)


def dot(a, b):
    return jnp.dot(a, b, preferred_element_type=F32)


def table_times(table, values):
    high, low = split(values)
    width = values.shape[1]
    both = dot(table[0], jnp.concatenate([high, low], axis=1))
    return both[:, :width] + (both[:, width:] + dot(table[1], high))


def times_table(values, table):
    high, low = split(values)
    return dot(high, table[0]) + (dot(low, table[0]) + dot(high, table[1]))


def step_kernel(
    slabs, counts, strength, offsets, cells, ambient, *refs,
):
    tables_in, (vel_out, vorticity_out) = refs[:9], refs[9:11]
    (
        packet, wide_x, high_y, low_y, charge, high_l, low_l, rim, rim_in, vort, vel, vorticity,
        plane_in, side, side_in, ys, xr, xo, zr, spec, zo, xr2, xo2, yr, fixed, row_swap, lane_swap,
    ) = refs[11:38]
    tables_here = refs[38:47]
    ahead_y, back_y, ahead_x, back_x, ahead_1, back_1, ahead_2, back_2, twiddle = tables_here
    (
        send_sem, recv_sem, own_sem, packet_send, packet_recv, rim_send, rim_recv,
        plane_send, plane_recv, side_send, side_recv, load_sem, store_sem,
    ) = refs[47:]
    me_z, me_x = lax.axis_index("gz"), lax.axis_index("gx")
    nx, nz = 4 * slabs, 8 * slabs
    xl = nx // PENCILS
    half = 4 * slabs
    part = 2 * xl
    wide = PLANES * MODES

    barrier = pltpu.get_barrier_semaphore()

    def greet(i, carry):
        pl.semaphore_signal(barrier, inc=1, device_id={"gz": lax.rem(me_z + i, slabs)}, device_id_type=MESH)
        return carry

    lax.fori_loop(1, slabs, greet, 0)
    for i in range(1, PENCILS):
        pl.semaphore_signal(barrier, inc=1, device_id={"gx": lax.rem(me_x + i, PENCILS)}, device_id_type=MESH)
    load_mesh = pltpu.make_async_copy(ambient, vort, load_sem.at[9])
    load_mesh.start()
    loads = [pltpu.make_async_copy(a, b, load_sem.at[n]) for n, (a, b) in enumerate(zip(tables_in, tables_here))]
    for copy in loads:
        copy.start()

    lane_id = lax.broadcasted_iota(jnp.int32, (1, PART), 1)
    up, down = counts[0], counts[1]
    moves = jnp.where(lane_id < up, 1, jnp.where(lane_id < up + down, -1, 0))
    cell = cells[...]
    packet[:, OWN:OWN + PART] = jnp.concatenate(
        [
            strength[...],
            offsets[...],
            (cell // (xl * NY) + PLANES * moves).astype(F32),
            (cell % (xl * NY)).astype(F32),
        ],
        axis=0,
    )

    def weigh(lo, hi):
        size = hi - lo
        fields = packet[:, lo:hi]
        lane = lax.broadcasted_iota(jnp.int32, (1, size), 1) + lo
        shift = jnp.where(lane < 128, -16.0, jnp.where(lane < OWN, -8.0, jnp.where(lane < OWN + PART, 0.0, jnp.where(lane < LANES - 128, 8.0, 16.0))))
        lateral = fields[7:8].astype(jnp.int32)
        plane = lax.broadcasted_iota(jnp.int32, (PLANES, size), 0).astype(F32)
        weight_z = kernel_weight((plane - (fields[6:7] + shift)) - fields[3:4])
        row = lax.broadcasted_iota(jnp.int32, (xl, size), 0).astype(F32)
        wide_x[:, lo:hi] = kernel_weight((row - (lateral >> 8).astype(F32)) - fields[4:5])
        at_y = lax.broadcasted_iota(jnp.int32, (NY, size), 0)
        away = ((at_y + (NY // 2 - (lateral & 255))) & 255) - NY // 2
        high, low = split(kernel_weight(away.astype(F32) - fields[5:6]))
        high_y[:, lo:hi] = high
        low_y[:, lo:hi] = low
        for c in range(3):
            charge[8 * c:8 * c + 8, lo:hi] = fields[c:c + 1] * weight_z

    weigh(OWN, OWN + PART)
    pl.semaphore_wait(barrier, slabs - 1 + PENCILS - 1)

    hops = []
    for n, (far, start, width, land) in enumerate(HOPS):
        hop = pltpu.make_async_remote_copy(
            src_ref=packet.at[:, OWN + start:OWN + start + width],
            dst_ref=packet.at[:, land:land + width],
            send_sem=packet_send.at[n],
            recv_sem=packet_recv.at[n],
            device_id={"gz": lax.rem(me_z + far + slabs, slabs)},
            device_id_type=MESH,
        )
        hop.start()
        hops.append(hop)

    def send_gx(src, dst, k, stage):
        mine = pl.ds(pl.multiple_of(me_x * part, 8), part)
        for i in (2, 1, 3):
            other = lax.rem(me_x + i, PENCILS)
            pltpu.make_async_remote_copy(
                src_ref=src.at[k, pl.ds(pl.multiple_of(other * part, 8), part)],
                dst_ref=dst.at[k, mine],
                send_sem=send_sem.at[stage, k],
                recv_sem=recv_sem.at[stage, k],
                device_id={"gx": other},
                device_id_type=MESH,
            ).start()
        own_copy(src, dst, k, stage).start()

    def send_gz(src, dst, k, stage):
        mine = pl.ds(pl.multiple_of(me_z * 8, 8), 8)

        def one(i, carry):
            other = lax.rem(me_z + i, slabs)
            pltpu.make_async_remote_copy(
                src_ref=src.at[k, pl.ds(pl.multiple_of(other * 8, 8), 8)],
                dst_ref=dst.at[k, mine],
                send_sem=send_sem.at[stage, k],
                recv_sem=recv_sem.at[stage, k],
                device_id={"gz": other},
                device_id_type=MESH,
            ).start()
            return carry

        lax.fori_loop(1, slabs, one, 0)
        own_copy(src, dst, k, stage).start()

    def own_copy(src, dst, k, stage):
        width, index = (part, me_x) if stage in (0, 3) else (8, me_z)
        at = pl.ds(pl.multiple_of(index * width, 8), width)
        return pltpu.make_async_copy(src.at[k, at], dst.at[k, at], own_sem.at[stage, k])

    def remote_rows(stage):
        return part * (PENCILS - 1) if stage in (0, 3) else 8 * (slabs - 1)

    def arrive(src, dst, k, stage):
        window = dst.at[k, pl.ds(0, remote_rows(stage))]
        pltpu.make_async_copy(window, window, recv_sem.at[stage, k]).wait()
        own_copy(src, dst, k, stage).wait()

    def sent(src, k, stage):
        window = src.at[k, pl.ds(0, remote_rows(stage))]
        pltpu.make_async_copy(window, window, send_sem.at[stage, k]).wait()

    for hop in hops:
        hop.wait_recv()
    weigh(0, OWN)
    weigh(OWN + PART, LANES)

    def spread_over_y(high, low, lo, hi):
        def times(a, b):
            return lax.dot_general(a, b, (((1,), (1,)), ((), ())), preferred_element_type=F32)

        top = high_y[:, lo:hi]
        return times(high, top) + (times(low, top) + times(high, low_y[:, lo:hi]))

    rims = []
    x_cell = (packet[7:8, :].astype(jnp.int32) >> 8).astype(F32)
    for n, first in enumerate((xl, -2)):
        beyond = [kernel_weight((float(first + r) - x_cell) - packet[4:5, :]) for r in range(2)]
        high, low = split(jnp.concatenate([charge[8 * c:8 * c + 8, :] * beyond[r] for c in range(3) for r in range(2)], axis=0))
        rim[n] = spread_over_y(high, low, 0, LANES)
        far = 1 if n == 0 else PENCILS - 1
        copy = pltpu.make_async_remote_copy(
            src_ref=rim.at[n],
            dst_ref=rim_in.at[n],
            send_sem=rim_send.at[n],
            recv_sem=rim_recv.at[n],
            device_id={"gx": lax.rem(me_x + far, PENCILS)},
            device_id_type=MESH,
        )
        copy.start()
        rims.append(copy)
    load_mesh.wait()

    def deposit(c):
        for planes, lo, hi in ((range(0, 2), 0, 1280), (range(2, 6), 512, 1280), (range(6, 8), 512, 1792)):
            columns = wide_x[:, lo:hi]
            for n, z in enumerate(planes):
                high, low = split(columns * charge[8 * c + z:8 * c + z + 1, lo:hi])
                high_l[n * xl:(n + 1) * xl, 0:hi - lo] = high
                low_l[n * xl:(n + 1) * xl, 0:hi - lo] = low
            size = len(planes) * xl
            at = planes[0] * xl
            vort[c, at:at + size] += spread_over_y(high_l[0:size, 0:hi - lo], low_l[0:size, 0:hi - lo], lo, hi)
        if c == 0:
            for copy in rims:
                copy.wait_recv()
        for n, first in enumerate((0, xl - 2)):
            for r in range(2):
                for z in range(PLANES):
                    at = c * 16 + r * 8 + z
                    to = z * xl + first + r
                    vort[c, to:to + 1, :] += rim_in[n, at:at + 1, :]

    spot = lax.broadcasted_iota(jnp.int32, (xl, wide), 1) >> 4
    for c in range(3):
        deposit(c)
        if c == 0:
            loads[0].wait()
        modes = times_table(vort[c], ahead_y)
        for p in range(2):
            turned = []
            for z in range(PLANES):
                tile = modes[z * xl:(z + 1) * xl, p * wide:(p + 1) * wide]
                turned.append(pltpu.roll(tile, MODES * z, 1) if z else tile)
            for q in range(8):
                picked = turned[0]
                for z in range(1, PLANES):
                    picked = jnp.where(spot == (q + z) % 8, turned[z], picked)
                if q:
                    picked = pltpu.roll(picked, wide - MODES * q, 1)
                at = (q % PENCILS) * part + p * xl
                ys[3 * (q // PENCILS) + c, at:at + xl] = picked
        send_gx(ys, xr, c, 0)
    for c in range(3):
        send_gx(ys, xr, 3 + c, 0)
    loads[2].wait()
    for k in range(CHUNKS):
        arrive(ys, xr, k, 0)
        xo[k] = table_times(ahead_x, xr[k])
        send_gz(xo, zr, k, 1)
    row = lax.broadcasted_iota(jnp.int32, (half, wide), 0)
    lane = lax.broadcasted_iota(jnp.int32, (half, wide), 1)
    slot = row & 3
    k1 = row >> 2
    kz = k1 + slabs * (lane >> 4)
    kx = 2 * me_z + (slot & 1)
    kx = jnp.where(slot >= 2, -kx, kx)
    kx = jnp.where((slot == 2) & (me_z == 0), nx // 2, kx)
    wave_z = jnp.where(kz < nz // 2, kz, kz - nz).astype(F32) * (2.0 * math.pi / nz)
    wave_x = kx.astype(F32) * (2.0 * math.pi / nx)
    flat_sq = wave_z * wave_z + wave_x * wave_x
    fixed[0] = jnp.where(kz == nz // 2, 0.0, wave_z)
    fixed[1] = jnp.where(kx == nx // 2, 0.0, wave_x)
    for h in range(2):
        ky = me_x * (2 * MODES) + h * MODES + (lane & 15)
        wave_y = ky.astype(F32) * (2.0 * math.pi / NY)
        anchor = (kz == 0) & (kx == 0) & (ky == 0)
        inverse = jnp.where(anchor, 0.0, 1.0 / jnp.where(anchor, 1.0, flat_sq + wave_y * wave_y))
        fixed[2 + 2 * h] = wave_y
        if h == 0:
            packed = ky == 0
            other = 1.0 / (flat_sq + math.pi * math.pi)
            fixed[6] = jnp.where(packed, 0.5 * (inverse - other), 0.0)
            inverse = jnp.where(packed, 0.5 * (inverse + other), inverse)
        fixed[3 + 2 * h] = inverse
    fro = lax.broadcasted_iota(jnp.int32, (half, half), 1)
    to = lax.broadcasted_iota(jnp.int32, (half, half), 0)
    to_slot = to & 3
    paired_slot = jnp.where(me_z == 0, jnp.where((to_slot & 1) == 0, to_slot, 4 - to_slot), (to_slot + 2) & 3)
    mirror_row = ((slabs - (to >> 2)) & (slabs - 1)) * KXS + paired_slot
    row_swap[...] = jnp.where(fro == mirror_row, 1.0, 0.0).astype(BF16)
    fro = lax.broadcasted_iota(jnp.int32, (2 * wide, 2 * wide), 0)
    to = lax.broadcasted_iota(jnp.int32, (2 * wide, 2 * wide), 1)
    mirror_lane = (to & wide) + (PLANES - 1 - ((to & (wide - 1)) >> 4)) * MODES
    sign = jnp.where(to < wide, 1.0, -1.0)
    lane_swap[...] = jnp.where((fro == mirror_lane) & ((to & 15) == 0), sign, 0.0).astype(BF16)
    for n in (4, 6, 8, 7, 5):
        loads[n].wait()

    def to_modes(k):
        mixed = table_times(ahead_1, zr[k])
        real, imag = mixed[:half], mixed[half:]
        cos_t, sin_t = twiddle[0], twiddle[1]
        turned = jnp.concatenate([real * cos_t + imag * sin_t, imag * cos_t - real * sin_t], axis=1)
        spec[k] = times_table(turned, ahead_2)

    def from_modes(k, real, imag):
        turned = times_table(jnp.concatenate([real, imag], axis=1), back_2)
        cos_t, sin_t = twiddle[0], twiddle[1]
        real, imag = turned[:, :wide], turned[:, wide:]
        mixed = jnp.concatenate([real * cos_t - imag * sin_t, imag * cos_t + real * sin_t], axis=0)
        zo[k] = table_times(back_1, mixed)

    def mirrored(k):
        high, low = split(spec[k])
        swapped = dot(row_swap[...], high) + dot(row_swap[...], low)
        high, low = split(swapped)
        swapped = dot(high, lane_swap[...]) + dot(low, lane_swap[...])
        parts = []
        for p in range(2):
            tile = swapped[:, p * wide:(p + 1) * wide]
            parts.append(jnp.where(k1 == 0, pltpu.roll(tile, MODES, 1), tile))
        return parts

    for h in range(2):
        for c in range(3):
            k = 3 * h + c
            arrive(xo, zr, k, 1)
            to_modes(k)
            if h == 0:
                pair = mirrored(k)
                for p in range(2):
                    at = slice(p * wide, (p + 1) * wide)
                    spec[k, :, at] = fixed[3] * spec[k, :, at] + fixed[6] * pair[p]
            else:
                for p in range(2):
                    at = slice(p * wide, (p + 1) * wide)
                    spec[k, :, at] = fixed[5] * spec[k, :, at]

        def stream(c, p):
            return spec[3 * h + c, :, p * wide:(p + 1) * wide]

        def curl(c, p):
            if c == 0:
                return fixed[1] * stream(2, p) - fixed[2 + 2 * h] * stream(1, p)
            if c == 1:
                return fixed[2 + 2 * h] * stream(0, p) - fixed[0] * stream(2, p)
            return fixed[0] * stream(1, p) - fixed[1] * stream(0, p)

        for c in range(3):
            from_modes(3 * h + c, -curl(c, 1), curl(c, 0))
            send_gz(zo, xr2, 3 * h + c, 2)
    loads[3].wait()
    for k in range(CHUNKS):
        arrive(zo, xr2, k, 2)
        xo2[k] = table_times(back_x, xr2[k])
        send_gx(xo2, yr, k, 3)
    loads[1].wait()
    edges = [[], [], []]
    stores = []
    at_x = lax.broadcasted_iota(jnp.int32, (xl, NY), 0)

    def stretch(c):
        for copy in edges[c]:
            copy.wait_recv()
        for z in range(PLANES):
            rows = slice(z * xl, (z + 1) * xl)
            here = vel[c, rows]
            above = vel[c, (z + 1) * xl:(z + 2) * xl] if z < PLANES - 1 else plane_in[1, c]
            below = vel[c, (z - 1) * xl:z * xl] if z > 0 else plane_in[0, c]
            right = jnp.where(at_x == xl - 1, side_in[1, c, z:z + 1, :], pltpu.roll(here, xl - 1, 0))
            left = jnp.where(at_x == 0, side_in[0, c, z:z + 1, :], pltpu.roll(here, 1, 0))
            along_y = pltpu.roll(here, NY - 1, 1) - pltpu.roll(here, 1, 1)
            rate = (
                vort[0, rows] * ((above - below) * 0.5)
                + vort[1, rows] * ((right - left) * 0.5)
                + vort[2, rows] * (along_y * 0.5)
            )
            vorticity[c, rows] = vort[c, rows] + 0.25 * rate
        stores.append(pltpu.make_async_copy(vorticity.at[c], vorticity_out.at[c], store_sem.at[1, c]))
        stores[-1].start()

    for c in range(3):
        rolled = []
        for q in range(8):
            h, b = q // PENCILS, q % PENCILS
            if b == 0:
                arrive(xo2, yr, 3 * h + c, 3)
            both = []
            for p in range(2):
                at = b * part + p * xl
                tile = yr[3 * h + c, at:at + xl]
                both.append(pltpu.roll(tile, MODES * q, 1) if q else tile)
            rolled.append(both)
        planes = []
        for z in range(PLANES):
            both = []
            for p in range(2):
                picked = rolled[0][p]
                for q in range(1, 8):
                    picked = jnp.where(spot == (q + z) % 8, rolled[q][p], picked)
                both.append(pltpu.roll(picked, wide - MODES * z, 1) if z else picked)
            planes.append(jnp.concatenate(both, axis=1))
        vel[c] = times_table(jnp.concatenate(planes, axis=0), back_y)
        for n, (far, z) in enumerate(((1, PLANES - 1), (slabs - 1, 0))):
            copy = pltpu.make_async_remote_copy(
                src_ref=vel.at[c, pl.ds(z * xl, xl)],
                dst_ref=plane_in.at[n, c],
                send_sem=plane_send.at[n, c],
                recv_sem=plane_recv.at[n, c],
                device_id={"gz": lax.rem(me_z + far, slabs)},
                device_id_type=MESH,
            )
            copy.start()
            edges[c].append(copy)
        for n, (far, x) in enumerate(((1, xl - 1), (PENCILS - 1, 0))):
            side[n, c] = jnp.concatenate([vel[c, z * xl + x:z * xl + x + 1, :] for z in range(PLANES)], axis=0)
            copy = pltpu.make_async_remote_copy(
                src_ref=side.at[n, c],
                dst_ref=side_in.at[n, c],
                send_sem=side_send.at[n, c],
                recv_sem=side_recv.at[n, c],
                device_id={"gx": lax.rem(me_x + far, PENCILS)},
                device_id_type=MESH,
            )
            copy.start()
            edges[c].append(copy)
        stores.append(pltpu.make_async_copy(vel.at[c], vel_out.at[c], store_sem.at[0, c]))
        stores[-1].start()
        if c:
            stretch(c - 1)
    stretch(2)
    for copy in hops + rims + edges[0] + edges[1] + edges[2]:
        copy.wait_send()
    for k in range(CHUNKS):
        sent(ys, k, 0)
        sent(xo, k, 1)
        sent(zo, k, 2)
        sent(xo2, k, 3)
    for copy in stores:
        copy.wait()


def on_device(strength, offsets, cell_index, migrate_count, ambient):
    slabs = lax.axis_size("gz")
    xl = ambient.shape[2]
    consts = [jnp.asarray(t) for t in tables(slabs)]
    chunk = pltpu.VMEM((CHUNKS, 8 * slabs, PLANES * MODES), F32)
    mesh = pltpu.VMEM((3, PLANES * xl, NY), F32)
    dma = pltpu.SemaphoreType.DMA
    vmem = pl.BlockSpec(memory_space=pltpu.VMEM)
    whole = pl.BlockSpec(memory_space=pl.ANY)
    flat = jax.ShapeDtypeStruct((3, PLANES * xl, NY), F32)
    velocity, vorticity = pl.pallas_call(
        functools.partial(step_kernel, slabs),
        out_shape=(flat, flat),
        in_specs=[pl.BlockSpec(memory_space=pltpu.SMEM), vmem, vmem, vmem, whole] + [whole] * len(consts),
        out_specs=(whole, whole),
        scratch_shapes=[
            pltpu.VMEM((8, LANES), F32),
            pltpu.VMEM((xl, LANES), F32),
            pltpu.VMEM((NY, LANES), BF16),
            pltpu.VMEM((NY, LANES), BF16),
            pltpu.VMEM((24, LANES), F32),
            pltpu.VMEM((4 * xl, 1280), BF16),
            pltpu.VMEM((4 * xl, 1280), BF16),
            pltpu.VMEM((2, 48, NY), F32),
            pltpu.VMEM((2, 48, NY), F32),
            mesh, mesh, mesh,
            pltpu.VMEM((2, 3, xl, NY), F32),
            pltpu.VMEM((2, 3, PLANES, NY), F32),
            pltpu.VMEM((2, 3, PLANES, NY), F32),
            chunk, chunk, chunk, chunk,
            pltpu.VMEM((CHUNKS, 4 * slabs, 2 * PLANES * MODES), F32),
            chunk, chunk, chunk, chunk,
            pltpu.VMEM((7, 4 * slabs, PLANES * MODES), F32),
            pltpu.VMEM((4 * slabs, 4 * slabs), BF16),
            pltpu.VMEM((2 * PLANES * MODES, 2 * PLANES * MODES), BF16),
            *[pltpu.VMEM(t.shape, t.dtype) for t in consts],
            dma((4, CHUNKS)), dma((4, CHUNKS)), dma((4, CHUNKS)),
            dma((6,)), dma((6,)), dma((2,)), dma((2,)),
            dma((2, 3)), dma((2, 3)), dma((2, 3)), dma((2, 3)),
            dma((10,)), dma((2, 3)),
        ],
        compiler_params=pltpu.CompilerParams(
            collective_id=0, has_side_effects=True, vmem_limit_bytes=57 * 1024 * 1024
        ),
    )(migrate_count.reshape(2), strength, offsets, cell_index.reshape(1, PART), ambient.reshape(flat.shape), *consts)
    return velocity.reshape(ambient.shape), vorticity.reshape(ambient.shape)


def solution(mesh):
    placed = (
        P(None, ("gz", "gx")),
        P(None, ("gz", "gx")),
        P(("gz", "gx")),
        P("gz", "gx", None),
        P(None, "gz", "gx", None),
    )
    return jax.shard_map(
        on_device,
        mesh=mesh,
        in_specs=placed,
        out_specs=(P(None, "gz", "gx", None), P(None, "gz", "gx", None)),
        check_vma=False,
    )
```

time: 137 us -> 118 us (0.86); the launches traced: 135 us -> 118 us
  Pallas kernels: 130 us -> 113 us
    pallas_call x1, Pallas kernels: 130 us -> 113 us  [on_device(): pl.pallas_call(functools.partial(step_kernel, slabs), out_shape=(flat, fl...]
where the time goes in v3:
time: 118 us
  Pallas kernels  113 us (96%)
  local copies, waits for them, and re-layouts  3.97 us (3%)
    pallas_call x1, Pallas kernels, on_device(): pl.pallas_call(functools.partial(step_kernel, slabs), out_shape=(flat, fl...  113 us
    unnamed x4, local copies, waits for them, and re-layouts  3.97 us

profile of v3, /device:TPU:8, one launch (start us, length us, event | category | flops | bytes accessed | tf_op | source)
XLA Modules:
  0.0 117.9 jit_solution(3212849151525220562)
XLA Ops:
  0.6 113.3 %shard_map.149 = (f32[3,512,256]{2,1,0:T(8,128)}, f32[3,512,256]{2,1,0:T(8,128)}) custom-call(s32[2]{0:T(128)} %bitcast.9, f32[3,512]{1,0:T(4,128)} %strength.1, f32[3,512]{1,0:T(4,128)} %offsets.1, s32[1,512]{1,0:T(1,128)} %bitcast.8, f32[3,512,256]{2,1,0:T(8,128)} %bitcast.7, bf16[2,256,256]{2,1,0:T(8,128)(2,1)} %constant.18.clone.refs_0_, ...), custom_call_target="tpu_custom_call" | custom-call | tf_op jit(solution)/shard_map/pallas_call | solution.py:511
  113.9 0.0 copy-start
  113.9 2.8 %copy.18 = f32[3,8,64,256]{3,2,1,0:T(8,128)} copy(f32[3,8,64,256]{3,2,1,0:T(8,128)} %bitcast.6) | data formatting | bytes 3145728
  116.7 0.0 copy-done
  116.7 1.1 copy.19
Async XLA Ops:
  113.9 2.8 %copy-start = (f32[3,512,256]{2,1,0:T(8,128)S(1)}, f32[3,512,256]{2,1,0:T(8,128)}, u32[]{:S(2)}) copy-start(f32[3,512,256]{2,1,0:T(8,128)} %get-tuple-element.5) | copy-start | bytes 4718596

commit v4 on v3

--- a/solution.py
+++ b/solution.py
@@ -20,6 +20,7 @@
 NY = 256
 PART = 512
 CHUNKS = 6
+GROUP = 9
 OWN = 640
 LANES = 1792
 HOPS = ((1, 0, 128, 512), (1, 128, 384, 128), (-1, 0, 128, 1152), (-1, 128, 384, 1280), (2, 0, 128, 0), (-2, 0, 128, 1664))
@@ -127,11 +128,20 @@
 
     barrier = pltpu.get_barrier_semaphore()
 
-    def greet(i, carry):
-        pl.semaphore_signal(barrier, inc=1, device_id={"gz": lax.rem(me_z + i, slabs)}, device_id_type=MESH)
-        return carry
-
-    lax.fori_loop(1, slabs, greet, 0)
+    def each_other_slab(act):
+        group = math.gcd(slabs - 1, GROUP)
+
+        def some(i, carry):
+            for j in range(group):
+                act(lax.rem(me_z + 1 + j + i * group, slabs))
+            return carry
+
+        lax.fori_loop(0, (slabs - 1) // group, some, 0)
+
+    def greet(other):
+        pl.semaphore_signal(barrier, inc=1, device_id={"gz": other}, device_id_type=MESH)
+
+    each_other_slab(greet)
     for i in range(1, PENCILS):
         pl.semaphore_signal(barrier, inc=1, device_id={"gx": lax.rem(me_x + i, PENCILS)}, device_id_type=MESH)
     load_mesh = pltpu.make_async_copy(ambient, vort, load_sem.at[9])
@@ -172,7 +182,6 @@
         for c in range(3):
             charge[8 * c:8 * c + 8, lo:hi] = fields[c:c + 1] * weight_z
 
-    weigh(OWN, OWN + PART)
     pl.semaphore_wait(barrier, slabs - 1 + PENCILS - 1)
 
     hops = []
@@ -205,8 +214,7 @@
     def send_gz(src, dst, k, stage):
         mine = pl.ds(pl.multiple_of(me_z * 8, 8), 8)
 
-        def one(i, carry):
-            other = lax.rem(me_z + i, slabs)
+        def one(other):
             pltpu.make_async_remote_copy(
                 src_ref=src.at[k, pl.ds(pl.multiple_of(other * 8, 8), 8)],
                 dst_ref=dst.at[k, mine],
@@ -215,9 +223,8 @@
                 device_id={"gz": other},
                 device_id_type=MESH,
             ).start()
-            return carry
-
-        lax.fori_loop(1, slabs, one, 0)
+
+        each_other_slab(one)
         own_copy(src, dst, k, stage).start()
 
     def own_copy(src, dst, k, stage):
@@ -237,6 +244,7 @@
         window = src.at[k, pl.ds(0, remote_rows(stage))]
         pltpu.make_async_copy(window, window, send_sem.at[stage, k]).wait()
 
+    weigh(OWN, OWN + PART)
     for hop in hops:
         hop.wait_recv()
     weigh(0, OWN)
@@ -408,36 +416,16 @@
             from_modes(3 * h + c, -curl(c, 1), curl(c, 0))
             send_gz(zo, xr2, 3 * h + c, 2)
     loads[3].wait()
-    for k in range(CHUNKS):
+    loads[1].wait()
+    edges = [[], [], []]
+    stores = []
+
+    def back_to_x(k):
         arrive(zo, xr2, k, 2)
         xo2[k] = table_times(back_x, xr2[k])
         send_gx(xo2, yr, k, 3)
-    loads[1].wait()
-    edges = [[], [], []]
-    stores = []
-    at_x = lax.broadcasted_iota(jnp.int32, (xl, NY), 0)
-
-    def stretch(c):
-        for copy in edges[c]:
-            copy.wait_recv()
-        for z in range(PLANES):
-            rows = slice(z * xl, (z + 1) * xl)
-            here = vel[c, rows]
-            above = vel[c, (z + 1) * xl:(z + 2) * xl] if z < PLANES - 1 else plane_in[1, c]
-            below = vel[c, (z - 1) * xl:z * xl] if z > 0 else plane_in[0, c]
-            right = jnp.where(at_x == xl - 1, side_in[1, c, z:z + 1, :], pltpu.roll(here, xl - 1, 0))
-            left = jnp.where(at_x == 0, side_in[0, c, z:z + 1, :], pltpu.roll(here, 1, 0))
-            along_y = pltpu.roll(here, NY - 1, 1) - pltpu.roll(here, 1, 1)
-            rate = (
-                vort[0, rows] * ((above - below) * 0.5)
-                + vort[1, rows] * ((right - left) * 0.5)
-                + vort[2, rows] * (along_y * 0.5)
-            )
-            vorticity[c, rows] = vort[c, rows] + 0.25 * rate
-        stores.append(pltpu.make_async_copy(vorticity.at[c], vorticity_out.at[c], store_sem.at[1, c]))
-        stores[-1].start()
-
-    for c in range(3):
+
+    def back_to_y(c):
         rolled = []
         for q in range(8):
             h, b = q // PENCILS, q % PENCILS
@@ -484,9 +472,48 @@
             edges[c].append(copy)
         stores.append(pltpu.make_async_copy(vel.at[c], vel_out.at[c], store_sem.at[0, c]))
         stores[-1].start()
-        if c:
-            stretch(c - 1)
-    stretch(2)
+
+    at_x = lax.broadcasted_iota(jnp.int32, (xl, NY), 0)
+
+    def stretch_inside(c):
+        for z in range(PLANES):
+            rows = slice(z * xl, (z + 1) * xl)
+            here = vel[c, rows]
+            along_z = -vel[c, (z - 1) * xl:z * xl] if z > 0 else None
+            if z < PLANES - 1:
+                above = vel[c, (z + 1) * xl:(z + 2) * xl]
+                along_z = above + along_z if z > 0 else above
+            right = jnp.where(at_x == xl - 1, 0.0, pltpu.roll(here, xl - 1, 0))
+            left = jnp.where(at_x == 0, 0.0, pltpu.roll(here, 1, 0))
+            along_y = pltpu.roll(here, NY - 1, 1) - pltpu.roll(here, 1, 1)
+            rate = vort[0, rows] * along_z + vort[1, rows] * (right - left) + vort[2, rows] * along_y
+            vorticity[c, rows] = vort[c, rows] + 0.125 * rate
+
+    def stretch_edges(c):
+        for copy in edges[c]:
+            copy.wait_recv()
+        for n, (first, sign) in enumerate(((0, -0.125), ((PLANES - 1) * xl, 0.125))):
+            rows = slice(first, first + xl)
+            vorticity[c, rows] += vort[0, rows] * (sign * plane_in[n, c])
+        for n, (first, sign) in enumerate(((0, -0.125), (xl - 1, 0.125))):
+            for z in range(PLANES):
+                at = z * xl + first
+                vorticity[c, at:at + 1, :] += vort[1, at:at + 1, :] * (sign * side_in[n, c, z:z + 1, :])
+        stores.append(pltpu.make_async_copy(vorticity.at[c], vorticity_out.at[c], store_sem.at[1, c]))
+        stores[-1].start()
+
+    for k in range(CHUNKS - 1):
+        back_to_x(k)
+    back_to_y(0)
+    back_to_x(CHUNKS - 1)
+    stretch_inside(0)
+    back_to_y(1)
+    stretch_edges(0)
+    stretch_inside(1)
+    back_to_y(2)
+    stretch_edges(1)
+    stretch_inside(2)
+    stretch_edges(2)
     for copy in hops + rims + edges[0] + edges[1] + edges[2]:
         copy.wait_send()
     for k in range(CHUNKS):
@@ -495,6 +522,17 @@
         sent(zo, k, 2)
         sent(xo2, k, 3)
     for copy in stores:
+        copy.wait()
+
+
+def put_kernel(velocity, vorticity, velocity_out, vorticity_out, sems):
+    copies = [
+        pltpu.make_async_copy(velocity, velocity_out, sems.at[0]),
+        pltpu.make_async_copy(vorticity, vorticity_out, sems.at[1]),
+    ]
+    for copy in copies:
+        copy.start()
+    for copy in copies:
         copy.wait()
 
 
@@ -510,7 +548,7 @@
     flat = jax.ShapeDtypeStruct((3, PLANES * xl, NY), F32)
     velocity, vorticity = pl.pallas_call(
         functools.partial(step_kernel, slabs),
-        out_shape=(flat, flat),
+        out_shape=(pltpu.VMEM(flat.shape, F32), pltpu.VMEM(flat.shape, F32)),
         in_specs=[pl.BlockSpec(memory_space=pltpu.SMEM), vmem, vmem, vmem, whole] + [whole] * len(consts),
         out_specs=(whole, whole),
         scratch_shapes=[
@@ -540,9 +578,16 @@
             dma((10,)), dma((2, 3)),
         ],
         compiler_params=pltpu.CompilerParams(
-            collective_id=0, has_side_effects=True, vmem_limit_bytes=57 * 1024 * 1024
+            collective_id=0, has_side_effects=True, vmem_limit_bytes=56 * 1024 * 1024
         ),
     )(migrate_count.reshape(2), strength, offsets, cell_index.reshape(1, PART), ambient.reshape(flat.shape), *consts)
+    velocity, vorticity = pl.pallas_call(
+        put_kernel,
+        out_shape=(flat, flat),
+        in_specs=[whole, whole],
+        out_specs=(whole, whole),
+        scratch_shapes=[dma((2,))],
+    )(velocity, vorticity)
     return velocity.reshape(ambient.shape), vorticity.reshape(ambient.shape)
 
 

time: 118 us -> 211 us (1.79)
  Pallas kernels: 113 us -> 208 us
    pallas_call x1 -> x2, Pallas kernels: 113 us -> 208 us  [the longest x1 111 us: on_device(): pl.pallas_call(functools.partial(step_kernel, slabs), out_shape=(pltpu.VM...]
where the time goes in v4:
time: 211 us
  Pallas kernels  208 us (99%)
  local copies, waits for them, and re-layouts  2.32 us (1%)
    pallas_call x1, Pallas kernels, on_device(): pl.pallas_call(functools.partial(step_kernel, slabs), out_shape=(pltpu.VM...  111 us
    pallas_call x1, Pallas kernels, on_device(): pl.pallas_call(put_kernel, out_shape=(flat, flat), in_specs=[whole, whole...  96.4 us

profile of v4, /device:TPU:8, one launch (start us, length us, event | category | flops | bytes accessed | tf_op | source)
XLA Modules:
  0.0 210.8 jit_solution(17199896464456835738)
XLA Ops:
  0.6 111.3 %shard_map.149 = (f32[3,512,256]{2,1,0:T(8,128)S(1)}, f32[3,512,256]{2,1,0:T(8,128)S(1)}) custom-call(s32[2]{0:T(128)} %bitcast.7, f32[3,512]{1,0:T(4,128)} %strength.1, f32[3,512]{1,0:T(4,128)} %offsets.1, s32[1,512]{1,0:T(1,128)} %bitcast.6, f32[3,512,256]{2,1,0:T(8,128)} %bitcast.5, bf16[2,256,256]{2,1,0:T(8,128)(2,1)} %constant.18.clone.refs_0_, ...), custom_call_target="tpu_custom_call" | custom-call | tf_op jit(solution)/shard_map/pallas_call | solution.py:549
  111.9 0.0 copy-start
  111.9 1.2 copy-done
  113.1 0.0 copy-start.1
  113.1 1.2 copy-done.1
  114.2 96.4 %shard_map.150 = (f32[3,512,256]{2,1,0:T(8,128)}, f32[3,512,256]{2,1,0:T(8,128)}) custom-call(f32[3,512,256]{2,1,0:T(8,128)} %copy-done, f32[3,512,256]{2,1,0:T(8,128)} %copy-done.1), custom_call_target="tpu_custom_call" | custom-call | tf_op jit(solution)/shard_map/pallas_call | solution.py:584
Async XLA Ops:
  111.9 1.2 copy-start
  113.1 1.2 copy-start.1

commit v5 on v4

--- a/solution.py
+++ b/solution.py
@@ -525,17 +525,6 @@
         copy.wait()
 
 
-def put_kernel(velocity, vorticity, velocity_out, vorticity_out, sems):
-    copies = [
-        pltpu.make_async_copy(velocity, velocity_out, sems.at[0]),
-        pltpu.make_async_copy(vorticity, vorticity_out, sems.at[1]),
-    ]
-    for copy in copies:
-        copy.start()
-    for copy in copies:
-        copy.wait()
-
-
 def on_device(strength, offsets, cell_index, migrate_count, ambient):
     slabs = lax.axis_size("gz")
     xl = ambient.shape[2]
@@ -581,13 +570,6 @@
             collective_id=0, has_side_effects=True, vmem_limit_bytes=56 * 1024 * 1024
         ),
     )(migrate_count.reshape(2), strength, offsets, cell_index.reshape(1, PART), ambient.reshape(flat.shape), *consts)
-    velocity, vorticity = pl.pallas_call(
-        put_kernel,
-        out_shape=(flat, flat),
-        in_specs=[whole, whole],
-        out_specs=(whole, whole),
-        scratch_shapes=[dma((2,))],
-    )(velocity, vorticity)
     return velocity.reshape(ambient.shape), vorticity.reshape(ambient.shape)
 
 

time: 211 us -> 115 us (0.55)
  Pallas kernels: 208 us -> 111 us
    pallas_call x1 -> x0, Pallas kernels: 96.4 us -> none  [on_device(): pl.pallas_call(put_kernel, out_shape=(flat, flat), in_specs=[whole, whole...]
where the time goes in v5:
time: 115 us; the launch traced here: 114 us
  Pallas kernels  111 us (97%)
  local copies, waits for them, and re-layouts  2.29 us (2%)
    pallas_call x1, Pallas kernels, on_device(): pl.pallas_call(functools.partial(step_kernel, slabs), out_shape=(pltpu.VM...  111 us

profile of v5, /device:TPU:8, one launch (start us, length us, event | category | flops | bytes accessed | tf_op | source)
XLA Modules:
  0.0 114.2 jit_solution(4783855528228917971)
XLA Ops:
  0.6 111.3 %shard_map.149 = (f32[3,512,256]{2,1,0:T(8,128)S(1)}, f32[3,512,256]{2,1,0:T(8,128)S(1)}) custom-call(s32[2]{0:T(128)} %bitcast.9, f32[3,512]{1,0:T(4,128)} %strength.1, f32[3,512]{1,0:T(4,128)} %offsets.1, s32[1,512]{1,0:T(1,128)} %bitcast.8, f32[3,512,256]{2,1,0:T(8,128)} %bitcast.7, bf16[2,256,256]{2,1,0:T(8,128)(2,1)} %constant.18.clone.refs_0_, ...), custom_call_target="tpu_custom_call" | custom-call | tf_op jit(solution)/shard_map/pallas_call | solution.py:538
  111.9 1.1 %copy.18 = f32[3,8,64,256]{3,2,1,0:T(8,128)} copy(f32[3,8,64,256]{3,2,1,0:T(8,128)S(1)} %bitcast.6) | data formatting | bytes 3145728
  113.1 1.1 copy.19

commit v6 on v5

--- a/solution.py
+++ b/solution.py
@@ -21,6 +21,7 @@
 PART = 512
 CHUNKS = 6
 GROUP = 9
+BLOCK = 32
 OWN = 640
 LANES = 1792
 HOPS = ((1, 0, 128, 512), (1, 128, 384, 128), (-1, 0, 128, 1152), (-1, 128, 384, 1280), (2, 0, 128, 0), (-2, 0, 128, 1664))
@@ -85,6 +86,9 @@
 
 
 def split(values):
+    if values.shape[0] > BLOCK:
+        pairs = [split(values[i:i + BLOCK]) for i in range(0, values.shape[0], BLOCK)]
+        return jnp.concatenate([a for a, _ in pairs], axis=0), jnp.concatenate([b for _, b in pairs], axis=0)
     high = values.astype(BF16)
     return high, (values - high.astype(F32)).astype(BF16)
 
@@ -172,13 +176,18 @@
         lateral = fields[7:8].astype(jnp.int32)
         plane = lax.broadcasted_iota(jnp.int32, (PLANES, size), 0).astype(F32)
         weight_z = kernel_weight((plane - (fields[6:7] + shift)) - fields[3:4])
-        row = lax.broadcasted_iota(jnp.int32, (xl, size), 0).astype(F32)
-        wide_x[:, lo:hi] = kernel_weight((row - (lateral >> 8).astype(F32)) - fields[4:5])
-        at_y = lax.broadcasted_iota(jnp.int32, (NY, size), 0)
-        away = ((at_y + (NY // 2 - (lateral & 255))) & 255) - NY // 2
-        high, low = split(kernel_weight(away.astype(F32) - fields[5:6]))
-        high_y[:, lo:hi] = high
-        low_y[:, lo:hi] = low
+        x_cell = (lateral >> 8).astype(F32)
+        block = min(xl, BLOCK)
+        for i in range(0, xl, block):
+            row = (lax.broadcasted_iota(jnp.int32, (block, size), 0) + i).astype(F32)
+            wide_x[i:i + block, lo:hi] = kernel_weight((row - x_cell) - fields[4:5])
+        start = NY // 2 - (lateral & 255)
+        for i in range(0, NY, 16):
+            at_y = lax.broadcasted_iota(jnp.int32, (16, size), 0) + i
+            away = ((at_y + start) & 255) - NY // 2
+            high, low = split(kernel_weight(away.astype(F32) - fields[5:6]))
+            high_y[i:i + 16, lo:hi] = high
+            low_y[i:i + 16, lo:hi] = low
         for c in range(3):
             charge[8 * c:8 * c + 8, lo:hi] = fields[c:c + 1] * weight_z
 
@@ -278,11 +287,14 @@
 
     def deposit(c):
         for planes, lo, hi in ((range(0, 2), 0, 1280), (range(2, 6), 512, 1280), (range(6, 8), 512, 1792)):
-            columns = wide_x[:, lo:hi]
-            for n, z in enumerate(planes):
-                high, low = split(columns * charge[8 * c + z:8 * c + z + 1, lo:hi])
-                high_l[n * xl:(n + 1) * xl, 0:hi - lo] = high
-                low_l[n * xl:(n + 1) * xl, 0:hi - lo] = low
+            block = min(xl, 16)
+            for i in range(0, xl, block):
+                columns = wide_x[i:i + block, lo:hi]
+                for n, z in enumerate(planes):
+                    high, low = split(columns * charge[8 * c + z:8 * c + z + 1, lo:hi])
+                    at = n * xl + i
+                    high_l[at:at + block, 0:hi - lo] = high
+                    low_l[at:at + block, 0:hi - lo] = low
             size = len(planes) * xl
             at = planes[0] * xl
             vort[c, at:at + size] += spread_over_y(high_l[0:size, 0:hi - lo], low_l[0:size, 0:hi - lo], lo, hi)
@@ -296,25 +308,27 @@
                     to = z * xl + first + r
                     vort[c, to:to + 1, :] += rim_in[n, at:at + 1, :]
 
-    spot = lax.broadcasted_iota(jnp.int32, (xl, wide), 1) >> 4
+    band = min(xl, 8)
+    spot = lax.broadcasted_iota(jnp.int32, (band, wide), 1) >> 4
     for c in range(3):
         deposit(c)
         if c == 0:
             loads[0].wait()
-        modes = times_table(vort[c], ahead_y)
+        vel[c] = times_table(vort[c], ahead_y)
         for p in range(2):
-            turned = []
-            for z in range(PLANES):
-                tile = modes[z * xl:(z + 1) * xl, p * wide:(p + 1) * wide]
-                turned.append(pltpu.roll(tile, MODES * z, 1) if z else tile)
-            for q in range(8):
-                picked = turned[0]
-                for z in range(1, PLANES):
-                    picked = jnp.where(spot == (q + z) % 8, turned[z], picked)
-                if q:
-                    picked = pltpu.roll(picked, wide - MODES * q, 1)
-                at = (q % PENCILS) * part + p * xl
-                ys[3 * (q // PENCILS) + c, at:at + xl] = picked
+            for i in range(0, xl, band):
+                turned = []
+                for z in range(PLANES):
+                    tile = vel[c, z * xl + i:z * xl + i + band, p * wide:(p + 1) * wide]
+                    turned.append(pltpu.roll(tile, MODES * z, 1) if z else tile)
+                for q in range(8):
+                    picked = turned[0]
+                    for z in range(1, PLANES):
+                        picked = jnp.where(spot == (q + z) % 8, turned[z], picked)
+                    if q:
+                        picked = pltpu.roll(picked, wide - MODES * q, 1)
+                    at = (q % PENCILS) * part + p * xl + i
+                    ys[3 * (q // PENCILS) + c, at:at + band] = picked
         send_gx(ys, xr, c, 0)
     for c in range(3):
         send_gx(ys, xr, 3 + c, 0)
@@ -426,27 +440,23 @@
         send_gx(xo2, yr, k, 3)
 
     def back_to_y(c):
-        rolled = []
-        for q in range(8):
-            h, b = q // PENCILS, q % PENCILS
-            if b == 0:
-                arrive(xo2, yr, 3 * h + c, 3)
-            both = []
-            for p in range(2):
-                at = b * part + p * xl
-                tile = yr[3 * h + c, at:at + xl]
-                both.append(pltpu.roll(tile, MODES * q, 1) if q else tile)
-            rolled.append(both)
-        planes = []
-        for z in range(PLANES):
-            both = []
-            for p in range(2):
-                picked = rolled[0][p]
-                for q in range(1, 8):
-                    picked = jnp.where(spot == (q + z) % 8, rolled[q][p], picked)
-                both.append(pltpu.roll(picked, wide - MODES * z, 1) if z else picked)
-            planes.append(jnp.concatenate(both, axis=1))
-        vel[c] = times_table(jnp.concatenate(planes, axis=0), back_y)
+        arrive(xo2, yr, c, 3)
+        arrive(xo2, yr, 3 + c, 3)
+        for p in range(2):
+            for i in range(0, xl, band):
+                turned = []
+                for q in range(8):
+                    at = (q % PENCILS) * part + p * xl + i
+                    tile = yr[3 * (q // PENCILS) + c, at:at + band]
+                    turned.append(pltpu.roll(tile, MODES * q, 1) if q else tile)
+                for z in range(PLANES):
+                    picked = turned[0]
+                    for q in range(1, 8):
+                        picked = jnp.where(spot == (q + z) % 8, turned[q], picked)
+                    if z:
+                        picked = pltpu.roll(picked, wide - MODES * z, 1)
+                    vel[c, z * xl + i:z * xl + i + band, p * wide:(p + 1) * wide] = picked
+        vel[c] = times_table(vel[c], back_y)
         for n, (far, z) in enumerate(((1, PLANES - 1), (slabs - 1, 0))):
             copy = pltpu.make_async_remote_copy(
                 src_ref=vel.at[c, pl.ds(z * xl, xl)],

time: 115 us -> 115 us (level)
  no operation moved by 1% of the time
where the time goes in v6:
time: 115 us; the launch traced here: 114 us
  Pallas kernels  111 us (97%)
  local copies, waits for them, and re-layouts  2.29 us (2%)
    pallas_call x1, Pallas kernels, on_device(): pl.pallas_call(functools.partial(step_kernel, slabs), out_shape=(pltpu.VM...  111 us

profile of v6, /device:TPU:8, one launch (start us, length us, event | category | flops | bytes accessed | tf_op | source)
XLA Modules:
  0.0 114.2 jit_solution(822340974381166585)
XLA Ops:
  0.6 111.2 %shard_map.149 = (f32[3,512,256]{2,1,0:T(8,128)S(1)}, f32[3,512,256]{2,1,0:T(8,128)S(1)}) custom-call(s32[2]{0:T(128)} %bitcast.9, f32[3,512]{1,0:T(4,128)} %strength.1, f32[3,512]{1,0:T(4,128)} %offsets.1, s32[1,512]{1,0:T(1,128)} %bitcast.8, f32[3,512,256]{2,1,0:T(8,128)} %bitcast.7, bf16[2,256,256]{2,1,0:T(8,128)(2,1)} %constant.18.clone.refs_0_, ...), custom_call_target="tpu_custom_call" | custom-call | tf_op jit(solution)/shard_map/pallas_call | solution.py:548
  111.9 1.1 %copy.18 = f32[3,8,64,256]{3,2,1,0:T(8,128)} copy(f32[3,8,64,256]{3,2,1,0:T(8,128)S(1)} %bitcast.6) | data formatting | bytes 3145728
  113.0 1.1 %copy.19 = f32[3,8,64,256]{3,2,1,0:T(8,128)} copy(f32[3,8,64,256]{3,2,1,0:T(8,128)S(1)} %bitcast.5) | data formatting | bytes 3145728

commit v7 on v6

--- a/solution.py
+++ b/solution.py
@@ -149,10 +149,7 @@
     for i in range(1, PENCILS):
         pl.semaphore_signal(barrier, inc=1, device_id={"gx": lax.rem(me_x + i, PENCILS)}, device_id_type=MESH)
     load_mesh = pltpu.make_async_copy(ambient, vort, load_sem.at[9])
-    load_mesh.start()
     loads = [pltpu.make_async_copy(a, b, load_sem.at[n]) for n, (a, b) in enumerate(zip(tables_in, tables_here))]
-    for copy in loads:
-        copy.start()
 
     lane_id = lax.broadcasted_iota(jnp.int32, (1, PART), 1)
     up, down = counts[0], counts[1]
@@ -253,6 +250,8 @@
         window = src.at[k, pl.ds(0, remote_rows(stage))]
         pltpu.make_async_copy(window, window, send_sem.at[stage, k]).wait()
 
+    load_mesh.start()
+    loads[0].start()
     weigh(OWN, OWN + PART)
     for hop in hops:
         hop.wait_recv()
@@ -284,6 +283,8 @@
         copy.start()
         rims.append(copy)
     load_mesh.wait()
+    for n in (2, 4, 6, 8, 7, 5, 3, 1):
+        loads[n].start()
 
     def deposit(c):
         for planes, lo, hi in ((range(0, 2), 0, 1280), (range(2, 6), 512, 1280), (range(6, 8), 512, 1792)):
@@ -308,6 +309,13 @@
                     to = z * xl + first + r
                     vort[c, to:to + 1, :] += rim_in[n, at:at + 1, :]
 
+    def to_x(k):
+        if k == 0:
+            loads[2].wait()
+        arrive(ys, xr, k, 0)
+        xo[k] = table_times(ahead_x, xr[k])
+        send_gz(xo, zr, k, 1)
+
     band = min(xl, 8)
     spot = lax.broadcasted_iota(jnp.int32, (band, wide), 1) >> 4
     for c in range(3):
@@ -330,13 +338,12 @@
                     at = (q % PENCILS) * part + p * xl + i
                     ys[3 * (q // PENCILS) + c, at:at + band] = picked
         send_gx(ys, xr, c, 0)
+        if c == 1:
+            to_x(0)
     for c in range(3):
         send_gx(ys, xr, 3 + c, 0)
-    loads[2].wait()
-    for k in range(CHUNKS):
-        arrive(ys, xr, k, 0)
-        xo[k] = table_times(ahead_x, xr[k])
-        send_gz(xo, zr, k, 1)
+    for k in range(1, CHUNKS):
+        to_x(k)
     row = lax.broadcasted_iota(jnp.int32, (half, wide), 0)
     lane = lax.broadcasted_iota(jnp.int32, (half, wide), 1)
     slot = row & 3

time: 115 us -> 112 us (0.974)
  Pallas kernels: 111 us -> 108 us
    pallas_call x1, Pallas kernels: 111 us -> 108 us  [on_device(): pl.pallas_call(functools.partial(step_kernel, slabs), out_shape=(pltpu.VM...]
where the time goes in v7:
time: 112 us; the launch traced here: 111 us
  Pallas kernels  108 us (96%)
  local copies, waits for them, and re-layouts  2.29 us (2%)
    pallas_call x1, Pallas kernels, on_device(): pl.pallas_call(functools.partial(step_kernel, slabs), out_shape=(pltpu.VM...  108 us
    unnamed x2, local copies, waits for them, and re-layouts  2.29 us

profile of v7, /device:TPU:8, one launch (start us, length us, event | category | flops | bytes accessed | tf_op | source)
XLA Modules:
  0.0 111.3 jit_solution(3696042382648433326)
XLA Ops:
  0.6 108.4 %shard_map.149 = (f32[3,512,256]{2,1,0:T(8,128)S(1)}, f32[3,512,256]{2,1,0:T(8,128)S(1)}) custom-call(s32[2]{0:T(128)} %bitcast.9, f32[3,512]{1,0:T(4,128)} %strength.1, f32[3,512]{1,0:T(4,128)} %offsets.1, s32[1,512]{1,0:T(1,128)} %bitcast.8, f32[3,512,256]{2,1,0:T(8,128)} %bitcast.7, bf16[2,256,256]{2,1,0:T(8,128)(2,1)} %constant.18.clone.refs_0_, ...), custom_call_target="tpu_custom_call" | custom-call | tf_op jit(solution)/shard_map/pallas_call | solution.py:555
  109.0 1.1 %copy.18 = f32[3,8,64,256]{3,2,1,0:T(8,128)} copy(f32[3,8,64,256]{3,2,1,0:T(8,128)S(1)} %bitcast.6) | data formatting | bytes 3145728
  110.1 1.1 %copy.19 = f32[3,8,64,256]{3,2,1,0:T(8,128)} copy(f32[3,8,64,256]{3,2,1,0:T(8,128)S(1)} %bitcast.5) | data formatting | bytes 3145728

commit v8 on v7

--- a/solution.py
+++ b/solution.py
@@ -110,7 +110,7 @@
 
 
 def step_kernel(
-    slabs, counts, strength, offsets, cells, ambient, *refs,
+    slabs, counts, strength_in, offsets_in, cells_in, ambient, *refs,
 ):
     tables_in, (vel_out, vorticity_out) = refs[:9], refs[9:11]
     (
@@ -121,7 +121,7 @@
     ahead_y, back_y, ahead_x, back_x, ahead_1, back_1, ahead_2, back_2, twiddle = tables_here
     (
         send_sem, recv_sem, own_sem, packet_send, packet_recv, rim_send, rim_recv,
-        plane_send, plane_recv, side_send, side_recv, load_sem, store_sem,
+        plane_send, plane_recv, side_send, side_recv, load_sem, store_sem, strength, offsets, cells,
     ) = refs[47:]
     me_z, me_x = lax.axis_index("gz"), lax.axis_index("gx")
     nx, nz = 4 * slabs, 8 * slabs
@@ -145,6 +145,12 @@
     def greet(other):
         pl.semaphore_signal(barrier, inc=1, device_id={"gz": other}, device_id_type=MESH)
 
+    small = [
+        pltpu.make_async_copy(a, b, load_sem.at[10 + n])
+        for n, (a, b) in enumerate(((strength_in, strength), (offsets_in, offsets), (cells_in, cells)))
+    ]
+    for copy in small:
+        copy.start()
     each_other_slab(greet)
     for i in range(1, PENCILS):
         pl.semaphore_signal(barrier, inc=1, device_id={"gx": lax.rem(me_x + i, PENCILS)}, device_id_type=MESH)
@@ -154,6 +160,8 @@
     lane_id = lax.broadcasted_iota(jnp.int32, (1, PART), 1)
     up, down = counts[0], counts[1]
     moves = jnp.where(lane_id < up, 1, jnp.where(lane_id < up + down, -1, 0))
+    for copy in small:
+        copy.wait()
     cell = cells[...]
     packet[:, OWN:OWN + PART] = jnp.concatenate(
         [
@@ -549,13 +557,12 @@
     chunk = pltpu.VMEM((CHUNKS, 8 * slabs, PLANES * MODES), F32)
     mesh = pltpu.VMEM((3, PLANES * xl, NY), F32)
     dma = pltpu.SemaphoreType.DMA
-    vmem = pl.BlockSpec(memory_space=pltpu.VMEM)
     whole = pl.BlockSpec(memory_space=pl.ANY)
     flat = jax.ShapeDtypeStruct((3, PLANES * xl, NY), F32)
     velocity, vorticity = pl.pallas_call(
         functools.partial(step_kernel, slabs),
         out_shape=(pltpu.VMEM(flat.shape, F32), pltpu.VMEM(flat.shape, F32)),
-        in_specs=[pl.BlockSpec(memory_space=pltpu.SMEM), vmem, vmem, vmem, whole] + [whole] * len(consts),
+        in_specs=[pl.BlockSpec(memory_space=pltpu.SMEM), whole, whole, whole, whole] + [whole] * len(consts),
         out_specs=(whole, whole),
         scratch_shapes=[
             pltpu.VMEM((8, LANES), F32),
@@ -581,7 +588,8 @@
             dma((4, CHUNKS)), dma((4, CHUNKS)), dma((4, CHUNKS)),
             dma((6,)), dma((6,)), dma((2,)), dma((2,)),
             dma((2, 3)), dma((2, 3)), dma((2, 3)), dma((2, 3)),
-            dma((10,)), dma((2, 3)),
+            dma((13,)), dma((2, 3)),
+            pltpu.VMEM((3, PART), F32), pltpu.VMEM((3, PART), F32), pltpu.VMEM((1, PART), jnp.int32),
         ],
         compiler_params=pltpu.CompilerParams(
             collective_id=0, has_side_effects=True, vmem_limit_bytes=56 * 1024 * 1024

time: 112 us -> 112 us (level)
  no operation moved by 1% of the time
where the time goes in v8:
time: 112 us; the launch traced here: 111 us
  Pallas kernels  108 us (96%)
  local copies, waits for them, and re-layouts  2.29 us (2%)
    pallas_call x1, Pallas kernels, on_device(): pl.pallas_call(functools.partial(step_kernel, slabs), out_shape=(pltpu.VM...  108 us
    unnamed x2, local copies, waits for them, and re-layouts  2.29 us

profile of v8, /device:TPU:8, one launch (start us, length us, event | category | flops | bytes accessed | tf_op | source)
XLA Modules:
  0.0 111.1 jit_solution(6953406218208165180)
XLA Ops:
  0.6 108.2 %shard_map.149 = (f32[3,512,256]{2,1,0:T(8,128)S(1)}, f32[3,512,256]{2,1,0:T(8,128)S(1)}) custom-call(s32[2]{0:T(128)} %bitcast.9, f32[3,512]{1,0:T(4,128)} %strength_in.1, f32[3,512]{1,0:T(4,128)} %offsets_in.1, s32[1,512]{1,0:T(1,128)} %bitcast.8, f32[3,512,256]{2,1,0:T(8,128)} %bitcast.7, bf16[2,256,256]{2,1,0:T(8,128)(2,1)} %constant.18.clone.refs_0_, ...), custom_call_target="tpu_custom_call" | custom-call | tf_op jit(solution)/shard_map/pallas_call | solution.py:562
  108.8 1.1 %copy.18 = f32[3,8,64,256]{3,2,1,0:T(8,128)} copy(f32[3,8,64,256]{3,2,1,0:T(8,128)S(1)} %bitcast.6) | data formatting | bytes 3145728
  110.0 1.1 %copy.19 = f32[3,8,64,256]{3,2,1,0:T(8,128)} copy(f32[3,8,64,256]{3,2,1,0:T(8,128)S(1)} %bitcast.5) | data formatting | bytes 3145728
